TPU v7x, 256 devices: a whole 4x4x8 slice. The times are simulated.
256 devices in a mesh: ens: 4 (over y), tile: 64 (over x, z, core).
Axes of the slice: x: 4, y: 4, z: 8, core: 2. Of those that a mesh axis runs over, the one named last changes fastest.
Arguments:
- surface: float32 [65536, 1024], P(('ens', 'tile')), parts along dimension 0, may hold values from -6 to 6
- flux_x: float32 [65536, 1024], P(('ens', 'tile')), parts along dimension 0, may hold values from -3 to 3
- flux_y: float32 [65536, 1024], P(('ens', 'tile')), parts along dimension 0, may hold values from -3 to 3
- celerity: float32 [65536, 1024], P(('ens', 'tile')), parts along dimension 0, may hold values from 0.05 to 0.45
- bed_depth: float32 [65536, 1024], P(('ens', 'tile')), parts along dimension 0, may hold values from 0.2 to 3
- roughness: float32 [65536, 1024], P(('ens', 'tile')), parts along dimension 0, may hold values from 0.2 to 2
- smoother: bfloat16 [256, 256], replicated, may hold values from -0.5 to 1.5
- block_plan: int32 [256, 4], P(('ens', 'tile')), parts along dimension 0, may hold values from 0 to 3, as said below
Outputs:
- new_surface: float32 [65536, 1024], P(('ens', 'tile')), parts along dimension 0
- new_flux_x: float32 [65536, 1024], P(('ens', 'tile')), parts along dimension 0
- new_flux_y: float32 [65536, 1024], P(('ens', 'tile')), parts along dimension 0
- resident: float32 [768, 2, 256, 256], P(('ens', 'tile')), parts along dimension 0
- energy: float32 [8], P('ens'), parts along dimension 0
There are 4 independent parts, one for each index of `ens`. A program takes and returns all parts, laid end to end along the dimension named above; an argument that names none is the same for every part. Nothing has to cross between parts.
Inputs may be any that keep to these rules, and one draw needn't show every extreme that they name: `block_plan`: codes per block: 0 dry, 1 to 3 wet with the slots of the steps. Every tile holds exactly one block of each code 1, 2 and 3 and one dry block, so every slot holds exactly one block.
All inputs are finite; a program needn't handle non-finite values.
Results may differ from a plain program's by a relative error of at most 0.022.
Values may be sent and summed in bfloat16 or wider, within the bound.
No kernel may reach another device: no remote copies, remote signals or barrier semaphores. Data moves between devices by JAX's collectives and lax.ppermute only.
A program may use at most 64 MiB of HBM per device.

v0:
```python
import jax
import jax.numpy as jnp
from jax import lax
from jax.sharding import PartitionSpec as P

STEPS = 2
SUB = 12


def passed_along(value, axis, steps):
    count = lax.axis_size(axis)
    leading, last = (max(0, -steps), min(count, count - steps))
    return lax.ppermute(value, axis, [(source, source + steps) for source in range(leading, last)])


def from_behind(block, axis, distance):
    devices = range(lax.axis_size(axis))
    route = [((i - distance) % len(devices), i) for i in devices]
    return lax.ppermute(block, axis, route)


def soften(packed, drag_ratio, smoother):
    weight = drag_ratio.astype(jnp.float32)[:, None]
    settled = jnp.zeros(packed.shape, jnp.float32)
    for _ in range(SUB):
        partial_rows = jnp.einsum(
            "sfij,kj->sfik", packed, smoother, preferred_element_type=jnp.float32
        ).astype(jnp.bfloat16)
        mixed_full = jnp.einsum(
            "ki,sfij->sfkj", smoother, partial_rows, preferred_element_type=jnp.float32
        )
        settled = mixed_full / (1.0 + weight * jnp.abs(mixed_full))
        packed = settled.astype(jnp.bfloat16)
    return settled


def choose(stacked, plan_codes, wanted):
    view_shape = (plan_codes.shape[0],) + (1,) * (stacked.ndim - 1)
    picked = jnp.where(
        (plan_codes == wanted).reshape(view_shape), stacked, jnp.zeros((), stacked.dtype)
    )
    return jnp.sum(picked, axis=0)


def on_device(surface, flux_x, flux_y, celerity, bed_depth, roughness, smoother, block_plan):
    row_count, col_count = surface.shape
    half_cols = col_count // 2
    block_side = smoother.shape[0]
    block_count = col_count // block_side
    tile_count = lax.axis_size("tile")
    position = lax.axis_index("tile")
    top_edge = position == 0
    bottom_edge = position == tile_count - 1
    col_ids = jnp.arange(col_count, dtype=jnp.int32)
    right_edge = (col_ids % half_cols == half_cols - 1)[None, :]
    left_edge = (col_ids % half_cols == 0)[None, :]
    plan_codes = block_plan[0]
    code_view = plan_codes.reshape(block_count, 1, 1, 1)
    level, flow_x, flow_y = (surface, flux_x, flux_y)
    resident = jnp.zeros((3, 2, block_side, block_side), jnp.float32)
    for repeat in range(STEPS):
        below_row = passed_along(level[0:1], "tile", -1)
        below_row = jnp.where(bottom_edge, 0.0, below_row)
        ahead_rows = jnp.concatenate([level[1:], below_row], 0)
        flow_x = flow_x - celerity * (ahead_rows - level)
        right_cells = jnp.where(right_edge, 0.0, jnp.roll(level, -1, axis=1))
        flow_y = flow_y - celerity * (right_cells - level)
        above_row = passed_along(flow_x[row_count - 1 :], "tile", 1)
        above_row = jnp.where(top_edge, 0.0, above_row)
        behind_x = jnp.concatenate([above_row, flow_x[:-1]], 0)
        behind_y = jnp.where(left_edge, 0.0, jnp.roll(flow_y, 1, axis=1))
        level = level - (flow_x - behind_x) - (flow_y - behind_y)
        drag_ratio = (roughness / jnp.maximum(level + bed_depth, 1.0)).astype(jnp.bfloat16)
        fluxes = jnp.stack([flow_x, flow_y], 0)
        flux_blocks = jnp.stack(
            [
                fluxes[:, :, column_index * block_side : (column_index + 1) * block_side]
                for column_index in range(block_count)
            ],
            0,
        )
        drag_blocks = jnp.stack(
            [
                drag_ratio[:, column_index * block_side : (column_index + 1) * block_side]
                for column_index in range(block_count)
            ],
            0,
        )
        payload = jnp.concatenate([flux_blocks.astype(jnp.bfloat16), drag_blocks[:, None]], 1)
        own_first = choose(payload, plan_codes, 1)
        go_near = choose(payload, plan_codes, 2)
        go_far = choose(payload, plan_codes, 3)
        got_near = from_behind(go_near, "tile", 1)
        got_far = from_behind(go_far, "tile", 2)
        slots = jnp.stack([own_first, got_near, got_far], 0)
        results = soften(slots[:, :2], slots[:, 2], smoother)
        home_near = from_behind(results[1], "tile", -1)
        home_far = from_behind(results[2], "tile", -2)
        new_blocks = jnp.where(
            code_view == 1,
            results[0],
            jnp.where(code_view == 2, home_near, jnp.where(code_view == 3, home_far, flux_blocks)),
        )
        resident = results
        flow_x = jnp.concatenate(
            [new_blocks[column_index, 0] for column_index in range(block_count)], 1
        )
        flow_y = jnp.concatenate(
            [new_blocks[column_index, 1] for column_index in range(block_count)], 1
        )
    total_rows = tile_count * row_count
    row_index = position * row_count + jnp.arange(row_count, dtype=jnp.int32)
    row_weight = 1.0 + 2.0 * row_index.astype(jnp.float32) / total_rows
    squares = (row_weight[:, None] * level * level).reshape(row_count, 2, half_cols)
    term_pair = jnp.sum(squares, axis=(0, 2)) / (total_rows * half_cols)
    energy = lax.psum(term_pair, "tile")
    return (level, flow_x, flow_y, resident, energy)


def solution(mesh):
    in_specs = (
        P(("ens", "tile"), None),
        P(("ens", "tile"), None),
        P(("ens", "tile"), None),
        P(("ens", "tile"), None),
        P(("ens", "tile"), None),
        P(("ens", "tile"), None),
        P(),
        P(("ens", "tile"), None),
    )
    out_specs = (
        P(("ens", "tile"), None),
        P(("ens", "tile"), None),
        P(("ens", "tile"), None),
        P(("ens", "tile"), None, None, None),
        P("ens"),
    )
    return jax.shard_map(
        on_device, mesh=mesh, in_specs=in_specs, out_specs=out_specs, check_vma=False
    )
```

profile of v0, /device:TPU:16, one launch (start us, length us, event | category | flops | bytes accessed | tf_op | source)
XLA Modules:
  0.0 310.2 jit_solution(10569381546483440016)
XLA Ops:
  5.7 2.5 fusion.94
  8.3 3.0 collective-permute-start.1
  17.5 2.1 collective-permute-start.3
  19.6 10.6 %collective-permute-done.2 = bf16[3,256,256]{2,1,0:T(8,128)(2,1)S(1)} collective-permute-done((bf16[3,256,256]{2,1,0:T(8,128)(2,1)S(1)}, bf16[3,256,256]{2,1,0:T(8,128)(2,1)S(1)}, u32[]{:S(2)}, u32[]{:S(2)}) %collective-permute-start.2) | collective-permute-done | bytes 393248 | tf_op jit(solution)/shard_map/ppermute | solution.py:19
  30.2 4.9 %collective-permute-done.3 = bf16[3,256,256]{2,1,0:T(8,128)(2,1)S(1)} collective-permute-done((bf16[3,256,256]{2,1,0:T(8,128)(2,1)S(1)}, bf16[3,256,256]{2,1,0:T(8,128)(2,1)S(1)}, u32[]{:S(2)}, u32[]{:S(2)}) %collective-permute-start.3) | collective-permute-done | bytes 393248 | tf_op jit(solution)/shard_map/ppermute | solution.py:19
  37.1 3.1 %fusion.48 = bf16[3,2,256,256]{2,3,1,0:T(8,128)(2,1)} fusion(bf16[1,3,256,256]{3,2,1,0:T(8,128)(2,1)} %bitcast.486, bf16[1,3,256,256]{3,2,1,0:T(8,128)(2,1)} %bitcast.482, bf16[1,3,256,256]{3,2,1,0:T(8,128)(2,1)} %bitcast.478, f32[3,256,256]{1,2,0:T(8,128)} %copy.32, bf16[256,256]{1,0:T(8,128)(2,1)S(1)} %copy-done), kind=kOutput, calls=%fused_computation.121 | convolution fusion | flops 408551424 | bytes 2883584 | tf_op jit(solution)/shard_map/ki,sfij->sfkj/dot_general | solution.py:29
  40.3 2.9 fusion.49
  43.2 2.9 fusion.50
  46.1 2.9 fusion.51
  49.0 2.9 fusion.52
  51.9 2.9 fusion.53
  54.8 2.9 fusion.54
  57.7 2.9 fusion.55
  60.6 2.9 fusion.56
  63.5 2.9 fusion.57
  66.4 2.9 fusion.58
  69.3 3.2 %bitcast_divide_fusion.12 = f32[3,2,256,256]{2,3,1,0:T(8,128)} fusion(bf16[3,2,256,256]{2,3,1,0:T(8,128)(2,1)} %fusion.58, f32[3,256,256]{1,2,0:T(8,128)S(1)} %copy-done.17, bf16[256,256]{1,0:T(8,128)(2,1)S(1)} %copy-done), kind=kOutput, calls=%fused_computation.66 | convolution fusion | flops 404619264 | bytes 3276800 | tf_op jit(solution)/shard_map/ki,sfij->sfkj/dot_general | solution.py:29
  72.4 2.6 slice_bitcast_fusion.5
  75.0 4.8 %collective-permute-start.4 = (f32[2,256,256]{1,2,0:T(8,128)}, f32[2,256,256]{1,2,0:T(8,128)}, u32[]{:S(2)}, u32[]{:S(2)}) collective-permute-start(f32[2,256,256]{1,2,0:T(8,128)} %get-tuple-element.63), channel_id=1, source_target_pairs={{1,0},{2,1},{3,2},{4,3},{5,4},{6,5},{7,6},{8,7},{9,8},{10,9},{11,1... | collective-permute-start | bytes 1572872 | tf_op jit(solution)/shard_map/ppermute | solution.py:19
  84.7 2.1 copy.55
  86.9 5.0 %collective-permute-done.4 = f32[2,256,256]{1,2,0:T(8,128)} collective-permute-done((f32[2,256,256]{1,2,0:T(8,128)}, f32[2,256,256]{1,2,0:T(8,128)}, u32[]{:S(2)}, u32[]{:S(2)}) %collective-permute-start.4) | collective-permute-done | bytes 524320 | tf_op jit(solution)/shard_map/ppermute | solution.py:19
  91.9 2.0 copy.56
  93.9 3.6 %collective-permute-done.5 = f32[2,256,256]{1,2,0:T(8,128)} collective-permute-done((f32[2,256,256]{1,2,0:T(8,128)}, f32[2,256,256]{1,2,0:T(8,128)}, u32[]{:S(2)}, u32[]{:S(2)}) %collective-permute-start.5) | collective-permute-done | bytes 524320 | tf_op jit(solution)/shard_map/ppermute | solution.py:19
  97.5 2.0 copy.57
  103.8 5.1 %collective-permute-start.7 = (f32[1,1024]{1,0:T(1,128)S(1)}, f32[1,1024]{1,0:T(1,128)S(1)}, u32[]{:S(2)}, u32[]{:S(2)}) collective-permute-start(f32[1,1024]{1,0:T(1,128)S(1)} %slice.259), channel_id=1, source_target_pairs={{0,1},{1,2},{2,3},{3,4},{4,5},{5,6},{6,7},{7,8},{8,9},{9,10},{10,1... | collective-permute-start | bytes 12296 | tf_op jit(solution)/shard_map/ppermute | solution.py:13
  115.4 12.2 %collective-permute-done.8 = bf16[3,256,256]{2,1,0:T(8,128)(2,1)S(1)} collective-permute-done((bf16[3,256,256]{2,1,0:T(8,128)(2,1)S(1)}, bf16[3,256,256]{2,1,0:T(8,128)(2,1)S(1)}, u32[]{:S(2)}, u32[]{:S(2)}) %collective-permute-start.8) | collective-permute-done | bytes 393248 | tf_op jit(solution)/shard_map/ppermute | solution.py:19
  130.9 3.0 fusion.59
  145.2 2.0 fusion.66
  152.8 2.3 bitcast_divide_fusion
  156.2 4.2 %collective-permute-start.10 = (f32[2,256,256]{1,2,0:T(8,128)}, f32[2,256,256]{1,2,0:T(8,128)}, u32[]{:S(2)}, u32[]{:S(2)}) collective-permute-start(f32[2,256,256]{1,2,0:T(8,128)} %get-tuple-element.60), channel_id=1, source_target_pairs={{1,0},{2,1},{3,2},{4,3},{5,4},{6,5},{7,6},{8,7},{9,8},{10,9},{11,1... | collective-permute-start | bytes 1572872 | tf_op jit(solution)/shard_map/ppermute | solution.py:19
  161.5 139.1 %psum.7 = f32[2]{0:T(128)} all-reduce(f32[2]{0:T(128)S(1)} %broadcast_multiply_fusion), channel_id=1, replica_groups=mesh['ens'=4,'tile'=64] {'tile'}, use_global_device_ids=true, to_apply=%region_8.9 | all-reduce | flops 2 | bytes 16 | tf_op jit(solution)/shard_map/psum | solution.py:116
  304.7 2.0 copy.85
  (118 shorter events, 58.1 us)
Async XLA Ops:
  0.6 36.5 %copy-start = (bf16[256,256]{1,0:T(8,128)(2,1)S(1)}, bf16[256,256]{1,0:T(8,128)(2,1)}, u32[]{:S(2)}) copy-start(bf16[256,256]{1,0:T(8,128)(2,1)} %param.14) | copy-start | bytes 393220
  0.6 4.2 %copy-start.1 = (f32[256,1024]{1,0:T(8,128)S(1)}, f32[256,1024]{1,0:T(8,128)}, u32[]{:S(2)}) copy-start(f32[256,1024]{1,0:T(8,128)} %param.8) | copy-start | bytes 3145732
  1.5 3.7 %collective-permute-start = (f32[1,1024]{1,0:T(1,128)S(1)}, f32[1,1024]{1,0:T(1,128)S(1)}, u32[]{:S(2)}, u32[]{:S(2)}) collective-permute-start(f32[1,1024]{1,0:T(1,128)S(1)} %slice.179), channel_id=1, source_target_pairs={{1,0},{2,1},{3,2},{4,3},{5,4},{6,5},{7,6},{8,7},{9,8},{10,9},{11,1... | collective-permute-start | bytes 12296 | tf_op jit(solution)/shard_map/ppermute | solution.py:13
  4.8 0.9 slice-start
  8.3 4.3 %collective-permute-start.1 = (f32[1,1024]{1,0:T(1,128)S(1)}, f32[1,1024]{1,0:T(1,128)S(1)}, u32[]{:S(2)}, u32[]{:S(2)}) collective-permute-start(f32[1,1024]{1,0:T(1,128)S(1)} %slice.236), channel_id=1, source_target_pairs={{0,1},{1,2},{2,3},{3,4},{4,5},{5,6},{6,7},{7,8},{8,9},{9,10},{10,1... | collective-permute-start | bytes 12296 | tf_op jit(solution)/shard_map/ppermute | solution.py:13
  11.5 1.0 copy-start.4
  11.6 1.6 copy-start.8
  11.6 1.9 copy-start.10
  15.9 19.3 %copy-start.16 = (bf16[3,256,256]{2,1,0:T(8,128)(2,1)}, bf16[3,256,256]{2,1,0:T(8,128)(2,1)S(1)}, u32[]{:S(2)}) copy-start(bf16[3,256,256]{2,1,0:T(8,128)(2,1)S(1)} %get-tuple-element.23) | copy-start | bytes 1179652
  15.9 14.3 %collective-permute-start.2 = (bf16[3,256,256]{2,1,0:T(8,128)(2,1)S(1)}, bf16[3,256,256]{2,1,0:T(8,128)(2,1)S(1)}, u32[]{:S(2)}, u32[]{:S(2)}) collective-permute-start(bf16[3,256,256]{2,1,0:T(8,128)(2,1)S(1)} %get-tuple-element.24), channel_id=1, source_target_pairs={{63,0},{0,1},{1,2},{2,3},{3,4},{4,5},{5,6},{6,7},{7,8},{8,9},{9,10... | collective-permute-start | bytes 1179656 | tf_op jit(solution)/shard_map/ppermute | solution.py:19
  17.5 17.6 %collective-permute-start.3 = (bf16[3,256,256]{2,1,0:T(8,128)(2,1)S(1)}, bf16[3,256,256]{2,1,0:T(8,128)(2,1)S(1)}, u32[]{:S(2)}, u32[]{:S(2)}) collective-permute-start(bf16[3,256,256]{2,1,0:T(8,128)(2,1)S(1)} %get-tuple-element.25), channel_id=1, source_target_pairs={{62,0},{63,1},{0,2},{1,3},{2,4},{3,5},{4,6},{5,7},{6,8},{7,9},{8,1... | collective-permute-start | bytes 1179656 | tf_op jit(solution)/shard_map/ppermute | solution.py:19
  30.2 4.9 %copy-start.19 = (bf16[3,256,256]{2,1,0:T(8,128)(2,1)}, bf16[3,256,256]{2,1,0:T(8,128)(2,1)S(1)}, u32[]{:S(2)}) copy-start(bf16[3,256,256]{2,1,0:T(8,128)(2,1)S(1)} %collective-permute-done.2) | copy-start | bytes 1179652
  37.1 3.2 %copy-start.17 = (f32[3,256,256]{1,2,0:T(8,128)S(1)}, f32[3,256,256]{1,2,0:T(8,128)}, u32[]{:S(2)}) copy-start(f32[3,256,256]{1,2,0:T(8,128)} %copy.32) | copy-start | bytes 2359300
  75.0 16.9 %collective-permute-start.4 = (f32[2,256,256]{1,2,0:T(8,128)}, f32[2,256,256]{1,2,0:T(8,128)}, u32[]{:S(2)}, u32[]{:S(2)}) collective-permute-start(f32[2,256,256]{1,2,0:T(8,128)} %get-tuple-element.63), channel_id=1, source_target_pairs={{1,0},{2,1},{3,2},{4,3},{5,4},{6,5},{7,6},{8,7},{9,8},{10,9},{11,1... | collective-permute-start | bytes 1572872 | tf_op jit(solution)/shard_map/ppermute | solution.py:19
  79.8 17.7 %collective-permute-start.5 = (f32[2,256,256]{1,2,0:T(8,128)}, f32[2,256,256]{1,2,0:T(8,128)}, u32[]{:S(2)}, u32[]{:S(2)}) collective-permute-start(f32[2,256,256]{1,2,0:T(8,128)} %get-tuple-element.62), channel_id=1, source_target_pairs={{2,0},{3,1},{4,2},{5,3},{6,4},{7,5},{8,6},{9,7},{10,8},{11,9},{12,... | collective-permute-start | bytes 1572872 | tf_op jit(solution)/shard_map/ppermute | solution.py:19
  80.8 3.9 %collective-permute-start.6 = (f32[1,1024]{1,0:T(1,128)S(1)}, f32[1,1024]{1,0:T(1,128)S(1)}, u32[]{:S(2)}, u32[]{:S(2)}) collective-permute-start(f32[1,1024]{1,0:T(1,128)S(1)} %slice.258), channel_id=1, source_target_pairs={{1,0},{2,1},{3,2},{4,3},{5,4},{6,5},{7,6},{8,7},{9,8},{10,9},{11,1... | collective-permute-start | bytes 12296 | tf_op jit(solution)/shard_map/ppermute | solution.py:13
  84.7 14.8 %copy-start.3 = (f32[1,2,256,256]{3,2,1,0:T(8,128)S(1)}, f32[1,2,256,256]{3,2,1,0:T(8,128)}, u32[]{:S(2)}) copy-start(f32[1,2,256,256]{3,2,1,0:T(8,128)} %copy-done.2) | copy-start | bytes 1572868
  84.7 14.8 %copy-start.5 = (f32[1,2,256,256]{3,2,1,0:T(8,128)S(1)}, f32[1,2,256,256]{3,2,1,0:T(8,128)}, u32[]{:S(2)}) copy-start(f32[1,2,256,256]{3,2,1,0:T(8,128)} %copy-done.4) | copy-start | bytes 1572868
  101.2 1.2 copy-start.13
  101.2 1.5 copy-start.14
  101.2 1.8 copy-start.15
  103.8 6.2 %collective-permute-start.7 = (f32[1,1024]{1,0:T(1,128)S(1)}, f32[1,1024]{1,0:T(1,128)S(1)}, u32[]{:S(2)}, u32[]{:S(2)}) collective-permute-start(f32[1,1024]{1,0:T(1,128)S(1)} %slice.259), channel_id=1, source_target_pairs={{0,1},{1,2},{2,3},{3,4},{4,5},{5,6},{6,7},{7,8},{8,9},{9,10},{10,1... | collective-permute-start | bytes 12296 | tf_op jit(solution)/shard_map/ppermute | solution.py:13
  109.1 0.8 copy-start.6
  110.0 1.2 copy-start.9
  110.0 1.5 copy-start.11
  110.7 1.1 copy-start.12
  113.5 14.2 %collective-permute-start.8 = (bf16[3,256,256]{2,1,0:T(8,128)(2,1)S(1)}, bf16[3,256,256]{2,1,0:T(8,128)(2,1)S(1)}, u32[]{:S(2)}, u32[]{:S(2)}) collective-permute-start(bf16[3,256,256]{2,1,0:T(8,128)(2,1)S(1)} %get-tuple-element.21), channel_id=1, source_target_pairs={{63,0},{0,1},{1,2},{2,3},{3,4},{4,5},{5,6},{6,7},{7,8},{8,9},{9,10... | collective-permute-start | bytes 1179656 | tf_op jit(solution)/shard_map/ppermute | solution.py:19
  113.6 15.3 %collective-permute-start.9 = (bf16[3,256,256]{2,1,0:T(8,128)(2,1)S(1)}, bf16[3,256,256]{2,1,0:T(8,128)(2,1)S(1)}, u32[]{:S(2)}, u32[]{:S(2)}) collective-permute-start(bf16[3,256,256]{2,1,0:T(8,128)(2,1)S(1)} %get-tuple-element.22), channel_id=1, source_target_pairs={{62,0},{63,1},{0,2},{1,3},{2,4},{3,5},{4,6},{5,7},{6,8},{7,9},{8,1... | collective-permute-start | bytes 1179656 | tf_op jit(solution)/shard_map/ppermute | solution.py:19
  130.9 3.0 copy-start.18
  156.2 147.2 %collective-permute-start.10 = (f32[2,256,256]{1,2,0:T(8,128)}, f32[2,256,256]{1,2,0:T(8,128)}, u32[]{:S(2)}, u32[]{:S(2)}) collective-permute-start(f32[2,256,256]{1,2,0:T(8,128)} %get-tuple-element.60), channel_id=1, source_target_pairs={{1,0},{2,1},{3,2},{4,3},{5,4},{6,5},{7,6},{8,7},{9,8},{10,9},{11,1... | collective-permute-start | bytes 1572872 | tf_op jit(solution)/shard_map/ppermute | solution.py:19
  160.5 144.3 %collective-permute-start.11 = (f32[2,256,256]{1,2,0:T(8,128)}, f32[2,256,256]{1,2,0:T(8,128)}, u32[]{:S(2)}, u32[]{:S(2)}) collective-permute-start(f32[2,256,256]{1,2,0:T(8,128)} %get-tuple-element.59), channel_id=1, source_target_pairs={{2,0},{3,1},{4,2},{5,3},{6,4},{7,5},{8,6},{9,7},{10,8},{11,9},{12,... | collective-permute-start | bytes 1572872 | tf_op jit(solution)/shard_map/ppermute | solution.py:19
  302.2 4.6 %copy-start.7 = (f32[1,2,256,256]{3,2,1,0:T(8,128)S(1)}, f32[1,2,256,256]{3,2,1,0:T(8,128)}, u32[]{:S(2)}) copy-start(f32[1,2,256,256]{3,2,1,0:T(8,128)} %copy-done.6) | copy-start | bytes 1572868
  (3 other events, 2.3 us)
where the time goes:
time: 316 us; the launch traced here: 310 us
  blocking collectives  139 us (44%)
  matrix products  59.5 us (19%)
  waiting for transfers between devices  37.6 us (12%)
  local copies, waits for them, and re-layouts  30.5 us (10%)
  starting transfers between devices  27.4 us (9%)
  other arithmetic  14.6 us (5%)
    psum x1, blocking collectives, on_device(): energy = lax.psum(term_pair, 'tile')  139 us
    dot_general x24, matrix products, soften(): jnp.einsum('ki,sfij->sfkj', smoother, partial_rows, preferred_element_typ...  59.5 us
    ppermute x8, waiting for transfers between devices, from_behind(): return lax.ppermute(block, axis, route)  37.6 us
    ppermute x8, starting transfers between devices, from_behind(): return lax.ppermute(block, axis, route)  16.5 us
    ppermute x4, starting transfers between devices, passed_along(): lax.ppermute(value, axis, [(source, source + steps) for source in range(l...  10.9 us
    unnamed x45, local copies, waits for them, and re-layouts  7.74 us
    ppermute x4, local copies, waits for them, and re-layouts, from_behind(): return lax.ppermute(block, axis, route)  7.34 us
    squeeze x4, local copies, waits for them, and re-layouts, on_device(): results[0]  7.17 us
  transfers between devices with their start and end apart: 12, of which 6 were waited for; matrix products, arithmetic and copies ran while one was open for 5% of the time, Pallas kernels for 0%

commit v1 on v0

v1 whole, which is shorter than its diff:
```python
import jax
import jax.numpy as jnp
from jax import lax
from jax.experimental import pallas as pl
from jax.experimental.pallas import tpu as pltpu
from jax.sharding import PartitionSpec as P

SUB = 12
EARLY = 6
EDGE = 8
PACK = 16
BAND = 32
GRANT = 16 * 2**20
F32 = jnp.float32
BF16 = jnp.bfloat16
VMEM = pl.BlockSpec(memory_space=pltpu.VMEM)
SMEM = pl.BlockSpec(memory_space=pltpu.SMEM)
HBM = pl.BlockSpec(memory_space=pltpu.HBM)


def shifted_left(rows, half):
    cols = rows.shape[1]
    ids = lax.broadcasted_iota(jnp.int32, rows.shape, 1) % half
    return jnp.where(ids == half - 1, 0.0, pltpu.roll(rows, cols - 1, 1))


def shifted_right(rows, half):
    ids = lax.broadcasted_iota(jnp.int32, rows.shape, 1) % half
    return jnp.where(ids == 0, 0.0, pltpu.roll(rows, 1, 1))


def drag_of(rough, level, depth):
    return (rough / jnp.maximum(level + depth, 1.0)).astype(BF16)


def code_column(plan, code, side):
    column = 0
    for k in range(plan.shape[1]):
        column = column + jnp.where(plan[0, k] == code, k * side, 0)
    return pl.multiple_of(column, side)


def advance(half, level, ahead, flow_x, flow_y, celerity, above_x):
    rows = level.shape[0]
    row_ids = lax.broadcasted_iota(jnp.int32, level.shape, 0)
    below = jnp.where(row_ids == rows - 1, ahead, pltpu.roll(level, rows - 1, 0))
    new_x = flow_x - celerity * (below - level)
    new_y = flow_y - celerity * (shifted_left(level, half) - level)
    behind_x = jnp.where(row_ids == 0, above_x, pltpu.roll(new_x, 1, 0))
    new_level = level - (new_x - behind_x) - (new_y - shifted_right(new_y, half))
    return new_x, new_y, new_level


def edge_rows(s, x, y, c, up, down, first, heads, tails, sems):
    rows = s.shape[0]
    copies = []
    for j, array in enumerate((s, x, y, c)):
        copies.append(pltpu.make_async_copy(array.at[pl.ds(0, EDGE)], heads.at[j], sems.at[2 * j]))
        copies.append(pltpu.make_async_copy(array.at[pl.ds(rows - EDGE, EDGE)], tails.at[j], sems.at[2 * j + 1]))
    for copy in copies:
        copy.start()
    for copy in copies:
        copy.wait()
    up[0:2] = heads[0, 0:2]
    for j in range(1, 4):
        up[j + 1:j + 2] = heads[j, 0:1]
    down[0:2] = tails[0, EDGE - 2:]
    down[2:4] = tails[1, EDGE - 2:]
    down[4:6] = tails[3, EDGE - 2:]
    down[6:7] = tails[2, EDGE - 1:]
    first[...] = heads[0, 0:1]


def first_step(s_in, x_in, y_in, c_in, b_in, r_in, sm_in, x_out, y_out, l_out, d_out, c, b, r, sm, sm_t,
               s, x, y, sems, sm_sem):
    total, cols = s.shape
    half = cols // 2
    bands = total // BAND
    pairs = ((s_in, s), (c_in, c), (x_in, x), (y_in, y), (b_in, b), (r_in, r))

    def copy(i, j):
        rows = pl.ds(i * BAND, BAND)
        source, target = pairs[j]
        return pltpu.make_async_copy(source.at[rows], target.at[rows], sems.at[i, j])

    sm_copy = pltpu.make_async_copy(sm_in, sm, sm_sem)
    sm_copy.start()
    for i in range(bands):
        for j in range(len(pairs)):
            copy(i, j).start()
    sm_copy.wait()
    sm_t[...] = sm[...].T
    above = jnp.zeros((1, cols), F32)
    for j in range(len(pairs)):
        copy(0, j).wait()
    for i in range(bands):
        rows = pl.ds(i * BAND, BAND)
        if i + 1 < bands:
            for j in range(len(pairs)):
                copy(i + 1, j).wait()
            ahead = s[pl.ds((i + 1) * BAND, 1)]
        else:
            ahead = jnp.zeros((1, cols), F32)
        new_x, new_y, level = advance(half, s[rows], ahead, x[rows], y[rows], c[rows], above)
        above = new_x[BAND - 1:]
        x_out[rows] = new_x
        y_out[rows] = new_y
        l_out[rows] = level
        d_out[rows] = drag_of(r[rows], level, b[rows])


def row_weight(shape, start, total_rows):
    ids = lax.broadcasted_iota(jnp.int32, shape, 0) + start
    return 1.0 + ids.astype(F32) * (2.0 / total_rows)


def second_step(tile_count, l_in, l_head, l_tail, halo, x_in, y_in, c, b, r, x_out, y_out, l_out, d_out, sums_out):
    total, cols = l_in.shape
    half = cols // 2
    bands = total // BAND
    position = lax.axis_index("tile")

    def level_band(i):
        start, stop = i * BAND, (i + 1) * BAND
        parts = [l_in[pl.ds(start, BAND)]]
        if i == 0:
            parts = [l_head[...], l_in[pl.ds(EDGE, BAND - EDGE)]]
        if i == bands - 1:
            parts = [l_in[pl.ds(start, BAND - EDGE)], l_tail[...]]
        return jnp.concatenate(parts, 0)

    above = jnp.zeros((1, cols), F32)
    sums = jnp.zeros((EDGE, cols), F32)
    level = level_band(0)
    for i in range(bands):
        rows = pl.ds(i * BAND, BAND)
        following = level_band(i + 1) if i + 1 < bands else halo[...]
        new_x, new_y, new_level = advance(half, level, following[0:1], x_in[rows], y_in[rows], c[rows], above)
        level = following
        above = new_x[BAND - 1:]
        x_out[rows] = new_x
        y_out[rows] = new_y
        l_out[rows] = new_level
        d_out[rows] = drag_of(r[rows], new_level, b[rows])
        for j in range(BAND // EDGE):
            if i + j > 0:
                part = new_level[j * EDGE:(j + 1) * EDGE]
                weight = row_weight(part.shape, position * total + i * BAND + j * EDGE, tile_count * total)
                sums = sums + weight * (part * part)
    sums_out[...] = sums


def second_edge(tile_count, row_count, down, halo, l_head, l2_head, sums, b_head, r_head, head, d_head, shares):
    cols = l_head.shape[1]
    half = cols // 2
    position = lax.axis_index("tile")
    total_rows = tile_count * row_count
    has_previous = jnp.where(position == 0, 0.0, 1.0)
    above_x = has_previous * (down[...] - halo[2:3] * (l_head[0:1] - halo[1:2]))
    row_ids = lax.broadcasted_iota(jnp.int32, (PACK, cols), 0)
    level = l2_head[...] + jnp.where(row_ids == 0, above_x, 0.0)
    head[...] = level
    d_head[...] = drag_of(r_head[...], level, b_head[...])
    top = level[:EDGE]
    whole = sums[...] + row_weight(top.shape, position * row_count, total_rows) * (top * top)
    lanes = lax.broadcasted_iota(jnp.int32, (1, 128), 1)
    share = jnp.zeros((1, 128), F32)
    for scenario in range(2):
        part = whole[:, scenario * half:(scenario + 1) * half]
        share = jnp.where(lanes == 2 * position + scenario, jnp.sum(part) * (1.0 / (total_rows * half)), share)
    shares[...] = share


def soften(smooth, smooth_t, held, drags, chains, repeats, put=None):
    for repeat in range(repeats):
        for chain in range(chains):
            mixed = jnp.dot(held[chain], smooth_t, preferred_element_type=F32).astype(BF16)
            full = jnp.dot(smooth, mixed, preferred_element_type=F32)
            settled = full / (1.0 + drags[chain // 2].astype(F32) * jnp.abs(full))
            if put is None or repeat + 1 < repeats:
                held[chain] = settled.astype(BF16)
            else:
                put(chain, settled)


def smooth_all(tile_count, plan, up, down, first, c, b, r, sm, sm_t, x_in, y_in, l_in, d_in,
               x, y, l_head, l_tail, halo, x_last, held, drags, edge):
    rows, cols = x.shape
    half = cols // 2
    side = sm.shape[0]
    position = lax.axis_index("tile")
    has_next = jnp.where(position == tile_count - 1, 0.0, 1.0)
    has_previous = jnp.where(position == 0, 0.0, 1.0)
    below = up[...] * has_next
    above = down[...] * has_previous
    tail, head = pl.ds(rows - EDGE, EDGE), pl.ds(0, EDGE)
    row_ids = lax.broadcasted_iota(jnp.int32, (EDGE, cols), 0)
    own_first = first[...]

    change = jnp.where(row_ids == EDGE - 1, c[tail] * below[0:1], 0.0)
    x_tail = x_in[tail] - change
    low = l_in[tail] + change
    l_tail[...] = low
    above_x = above[3:4] - above[5:6] * (own_first - above[1:2])
    top = l_in[head] + jnp.where(row_ids == 0, above_x, 0.0)
    l_head[...] = top

    next_x = below[2:3] - below[4:5] * (below[1:2] - below[0:1])
    next_y = below[3:4] - below[4:5] * (shifted_left(below[0:1], half) - below[0:1])
    next_level = below[0:1] - (next_x - x_tail[EDGE - 1:]) - (next_y - shifted_right(next_y, half))
    halo[0:1] = has_next * next_level
    before_x = above[2:3] - above[4:5] * (above[1:2] - above[0:1])
    before_y = above[6:7] - above[5:6] * (shifted_left(above[1:2], half) - above[1:2])
    halo[1:2] = above[1:2] - (above_x - before_x) - (before_y - shifted_right(before_y, half))
    halo[2:3] = above[5:6]

    first_rows, last_rows = pl.ds(0, PACK), pl.ds(rows - PACK, PACK)
    first_edge, last_edge = pl.ds(0, PACK), pl.ds(PACK, PACK)
    edge[first_edge] = drag_of(r[first_rows], jnp.concatenate([top, l_in[pl.ds(EDGE, EDGE)]], 0), b[first_rows])
    edge[last_edge] = drag_of(r[last_rows], jnp.concatenate([l_in[pl.ds(rows - PACK, EDGE)], low], 0), b[last_rows])
    x[...] = x_in[...]
    x[tail] = x_tail
    y[...] = y_in[...]
    columns = [code_column(plan, code, side) for code in (1, 2, 3)]
    for slot, column in enumerate(columns):
        span = pl.ds(column, side)
        drags[slot] = d_in[:, span]
        drags[slot, first_rows] = edge[first_edge, span]
        drags[slot, last_rows] = edge[last_edge, span]
        held[2 * slot] = x[:, span].astype(BF16)
        held[2 * slot + 1] = y[:, span].astype(BF16)

    def put(chain, settled):
        flux = (x, y)[chain % 2]
        flux[:, pl.ds(columns[chain // 2], side)] = settled

    soften(sm[...], sm_t[...], held, drags, 6, SUB, put)
    x_last[...] = x[rows - 1:rows]


def start_blocks(codes, plan, x, y, d, d_head, sm, sm_t, held, drags, edge):
    side = sm.shape[0]
    edge[...] = d_head[...]
    for slot, code in enumerate(codes):
        span = pl.ds(code_column(plan, code, side), side)
        drags[slot] = d[:, span]
        drags[slot, 0:PACK] = edge[:, span]
        held[2 * slot] = x[:, span].astype(BF16)
        held[2 * slot + 1] = y[:, span].astype(BF16)
    soften(sm[...], sm_t[...], held, drags, 2 * len(codes), EARLY)


def finish_sent(sm, sm_t, held_in, drags, settled_out, near, far, held):
    held[...] = held_in[...]

    def put(chain, settled):
        settled_out[chain // 2, chain % 2] = settled
        (near, far)[chain // 2][chain % 2] = settled.astype(BF16)

    soften(sm[...], sm_t[...], held, drags, 4, SUB - EARLY, put)


def finish_own(plan, sm, sm_t, held_in, drags, x_in, y_in, l_in, head, sent, x, y, lev, resident, held, stage, sems):
    side = sm.shape[0]
    rows = l_in.shape[0]
    blocks = plan.shape[1]
    places = [(code, pl.ds(code_column(plan, code, side), side)) for code in range(blocks)]
    outs = (x, y)
    copies = [
        (head.at[pl.ds(0, PACK)], lev.at[pl.ds(0, PACK)]),
        (l_in.at[pl.ds(PACK, rows - PACK)], lev.at[pl.ds(PACK, rows - PACK)]),
    ]
    late = [(stage, resident.at[0])]
    for code, span in places:
        for f in range(2):
            target = outs[f].at[:, span]
            if code == 0:
                copies.append(((x_in, y_in)[f].at[:, span], target))
            elif code == 1:
                late.append((stage.at[f], target))
            else:
                copies.append((sent.at[code - 2, f], target))
    started = [pltpu.make_async_copy(a, b, sems.at[i]) for i, (a, b) in enumerate(copies)]
    for copy in started:
        copy.start()
    held[...] = held_in[...]

    def put(chain, settled):
        stage[chain] = settled

    soften(sm[...], sm_t[...], held, drags, 2, SUB - EARLY, put)
    for i, (a, b) in enumerate(late):
        started.append(pltpu.make_async_copy(a, b, sems.at[len(copies) + i]))
        started[-1].start()
    for copy in started:
        copy.wait()


def settle_resident(near, far, held_resident, resident, stage, sems):
    copies = []
    for slot, block in enumerate((near, far)):
        stage[slot] = block[...].astype(F32)
        copies.append(pltpu.make_async_copy(stage.at[slot], resident.at[slot + 1], sems.at[slot]))
        copies[-1].start()
    for copy in copies:
        copy.wait()


def add_shares(mine, received, energy):
    shares = mine[...] + received[...]
    lanes = lax.broadcasted_iota(jnp.int32, shares.shape, 1)
    for scenario in range(2):
        energy[scenario] = jnp.sum(jnp.where(lanes % 2 == scenario, shares, 0.0))


def moved(value, steps):
    count = lax.axis_size("tile")
    return lax.ppermute(value, "tile", [(i, (i + steps) % count) for i in range(count)])


def exchange_stages(count):
    deep = 8 if count >= 16 else max(count // 2, 1)
    wide = count // (2 * deep)

    def index(x, z, core):
        return (x * deep + z) * 2 + core

    def stage(rule):
        pairs = []
        for i in range(count):
            core, z, x = i % 2, (i // 2) % deep, i // (2 * deep)
            pairs.append((i, index(*rule(x, z, core))))
        return pairs

    stages = []
    if deep == 8:
        across = {0: 6, 1: 7, 2: 4, 3: 5, 4: 2, 5: 3, 6: 0, 7: 1}
        stages.append(stage(lambda x, z, core: (x, z ^ 2, core)))
        stages.append(stage(lambda x, z, core: (x, z ^ 1, core)))
    else:
        reach = 1
        while reach < deep:
            stages.append(stage(lambda x, z, core, reach=reach: (x, z ^ reach, core)))
            reach *= 2
    if wide >= 2:
        stages.append(stage(lambda x, z, core: (x ^ 1, z, core)))
    if wide == 4:
        stages.append(stage(lambda x, z, core: (3 - x, z, core)))
    stages.append(stage(lambda x, z, core: (x, z, 1 - core)))
    if deep == 8:
        stages.append(stage(lambda x, z, core: (x, across[z], core)))
    return stages


def on_device(surface, flux_x, flux_y, celerity, bed_depth, roughness, smoother, plan):
    rows, cols = surface.shape
    side = smoother.shape[0]
    tiles = lax.axis_size("tile")

    def arr(*shape, dtype=F32):
        return jax.ShapeDtypeStruct(shape, dtype)

    field, square = arr(rows, cols), arr(side, side, dtype=BF16)
    drag = arr(rows, cols, dtype=BF16)

    def call(body, name, ins, outs, out_specs, operands, scratch=(), aliases={}, flops=0, moved_bytes=0):
        return pl.pallas_call(
            body,
            out_shape=outs,
            in_specs=ins,
            out_specs=out_specs,
            scratch_shapes=scratch,
            input_output_aliases=aliases,
            compiler_params=pltpu.CompilerParams(vmem_limit_bytes=GRANT),
            cost_estimate=pl.CostEstimate(flops=flops, bytes_accessed=moved_bytes, transcendentals=0),
            name=name,
        )(*operands)

    def dots(chains, repeats):
        return chains * repeats * 4 * side**3

    def squares(count):
        return pltpu.VMEM((count, side, side), BF16)

    def partner(value, pairs):
        return lax.ppermute(value, "tile", pairs)

    surface, flux_x, flux_y, celerity, bed_depth, roughness, smoother = [
        pltpu.with_memory_space_constraint(array, pltpu.HBM)
        for array in (surface, flux_x, flux_y, celerity, bed_depth, roughness, smoother)
    ]
    up, down, first = call(
        edge_rows, "edge_rows", [HBM] * 4, (arr(5, cols), arr(7, cols), arr(1, cols)), [VMEM] * 3,
        (surface, flux_x, flux_y, celerity),
        [pltpu.VMEM((4, EDGE, cols), F32)] * 2 + [pltpu.SemaphoreType.DMA((8,))])
    up = moved(up, -1)
    down = moved(down, 1)
    x, y, lev, d, c, b, r, sm, sm_t = call(
        first_step, "first_step", [HBM] * 7, (field, field, field, drag, field, field, field, square, square), [VMEM] * 9,
        (surface, flux_x, flux_y, celerity, bed_depth, roughness, smoother),
        [pltpu.VMEM((rows, cols), F32)] * 3 + [pltpu.SemaphoreType.DMA((rows // BAND, 6)), pltpu.SemaphoreType.DMA],
        flops=20 * rows * cols, moved_bytes=24 * rows * cols)
    x, y, l_head, l_tail, halo, x_last = call(
        lambda *refs: smooth_all(tiles, *refs), "smooth_all", [SMEM] + [VMEM] * 12,
        (field, field, arr(EDGE, cols), arr(EDGE, cols), arr(3, cols), arr(1, cols)), [VMEM] * 6,
        (plan, up, down, first, c, b, r, sm, sm_t, x, y, lev, d),
        [squares(6), squares(3), pltpu.VMEM((2 * PACK, cols), BF16)], flops=dots(6, SUB), moved_bytes=8 * rows * cols)
    down = moved(x_last, 1)
    x, y, lev, d, sums = call(
        lambda *refs: second_step(tiles, *refs), "second_step", [VMEM] * 9,
        (field, field, field, drag, arr(EDGE, cols)), [VMEM] * 5,
        (lev, l_head, l_tail, halo, x, y, c, b, r),
        flops=20 * rows * cols, moved_bytes=8 * rows * cols)
    head, d_head, shares = call(
        lambda *refs: second_edge(tiles, rows, *refs), "second_edge", [VMEM] * 7,
        (arr(PACK, cols), arr(PACK, cols, dtype=BF16), arr(1, 128)), [VMEM] * 3,
        (down, halo, l_head, lev[:PACK], sums, b[:PACK], r[:PACK]), flops=cols, moved_bytes=cols)

    stages = exchange_stages(tiles)
    done = 0
    met = partner(shares, stages[done])
    edge_scratch = [pltpu.VMEM((PACK, cols), BF16)]
    held, drags = call(
        lambda *refs: start_blocks((2, 3), *refs), "start_sent", [SMEM] + [VMEM] * 6,
        (arr(4, side, side, dtype=BF16), arr(2, side, side, dtype=BF16)), [VMEM] * 2,
        (plan, x, y, d, d_head, sm, sm_t), edge_scratch, flops=dots(4, EARLY), moved_bytes=rows * cols)

    def next_stage(shares, met, done, *after):
        shares = shares + met
        done += 1
        shares, *after = lax.optimization_barrier((shares,) + after)
        return shares, partner(shares, stages[done]), done, tuple(after)

    shares, met, done, (held,) = next_stage(shares, met, done, held)
    pair = arr(2, side, side, dtype=BF16)
    sent, near, far = call(
        finish_sent, "finish_sent", [VMEM] * 4, (arr(2, 2, side, side), pair, pair), [VMEM] * 3,
        (sm, sm_t, held, drags), [squares(4)], flops=dots(4, SUB - EARLY), moved_bytes=rows * cols)
    far = moved(far, 2)
    near = moved(near, 1)
    if done < len(stages) - 1:
        shares, met, done, (sent,) = next_stage(shares, met, done, sent)
    held, drags = call(
        lambda *refs: start_blocks((1,), *refs), "start_own", [SMEM] + [VMEM] * 6,
        (arr(2, side, side, dtype=BF16), arr(1, side, side, dtype=BF16)), [VMEM] * 2,
        (plan, x, y, d, d_head, sm, sm_t), edge_scratch, flops=dots(2, EARLY), moved_bytes=rows * cols)
    if done < len(stages) - 1:
        shares, met, done, (held,) = next_stage(shares, met, done, held)
    copies = 2 + 3 * (plan.shape[1] + 1)
    x, y, level, resident = call(
        finish_own, "finish_own", [SMEM] + [VMEM] * 9, (field, field, field, arr(3, 2, side, side)), [HBM] * 4,
        (plan, sm, sm_t, held, drags, x, y, lev, head, sent),
        [squares(2), pltpu.VMEM((2, side, side), F32), pltpu.SemaphoreType.DMA((copies,))],
        flops=dots(2, SUB - EARLY), moved_bytes=12 * rows * cols)
    if done < len(stages) - 1:
        shares, met, done, (resident,) = next_stage(shares, met, done, resident)
    while done < len(stages) - 1:
        shares, met, done, _ = next_stage(shares, met, done)
    resident = call(
        settle_resident, "settle_resident", [VMEM, VMEM, HBM], arr(3, 2, side, side), HBM,
        (near, far, resident),
        [pltpu.VMEM((2, 2, side, side), F32), pltpu.SemaphoreType.DMA((2,))],
        aliases={2: 0}, moved_bytes=24 * side * side)
    energy = call(add_shares, "add_shares", [VMEM] * 2, arr(2), SMEM, (shares, met))
    return level, x, y, resident, energy


def solution(mesh):
    cut = P(("ens", "tile"), None)
    return jax.shard_map(
        on_device,
        mesh=mesh,
        in_specs=(cut,) * 6 + (P(), cut),
        out_specs=(cut, cut, cut, P(("ens", "tile"), None, None, None), P("ens")),
        check_vma=False,
    )
```

time: 316 us -> 57.7 us (0.18); the launches traced: 310 us -> 56.8 us
  blocking collectives: 139 us -> 0 us
  matrix products: 59.5 us -> 0 us
  local copies, waits for them, and re-layouts: 30.5 us -> 0.03 us
  Pallas kernels: 0 us -> 26.7 us
  waiting for transfers between devices: 37.6 us -> 16.3 us
  starting transfers between devices: 27.4 us -> 12.8 us
  other arithmetic: 14.6 us -> 0.02 us
    psum x1 -> x0, blocking collectives: 139 us -> none  [on_device(): energy = lax.psum(term_pair, 'tile')]
    dot_general x24 -> x0, matrix products: 59.5 us -> none  [soften(): jnp.einsum('ki,sfij->sfkj', smoother, partial_rows, preferred_element_typ...]
    pallas_call x0 -> x11, Pallas kernels: none -> 26.7 us  [call(): pl.pallas_call(body, out_shape=outs, in_specs=ins, out_specs=out_specs, s...]
    ppermute x12 -> x11, waiting for transfers between devices: 37.6 us -> 16.3 us  [the longest x6 11.1 us: partner(): return lax.ppermute(value, 'tile', pairs)]
    ppermute x12 -> x11, starting transfers between devices: 27.4 us -> 12.8 us  [the longest x5 7.9 us: moved(): lax.ppermute(value, 'tile', [(i, (i + steps) % count) for i in range(coun...]
    unnamed x45 -> x2, local copies, waits for them, and re-layouts: 7.74 us -> 0.01 us
    squeeze x6 -> x0, local copies, waits for them, and re-layouts: 7.45 us -> none  [the longest x4 7.17 us: on_device(): results[0]]
    ppermute x4 -> x0, local copies, waits for them, and re-layouts: 7.34 us -> none  [from_behind(): return lax.ppermute(block, axis, route)]
  transfers between devices with their start and end apart: 12 -> 11, of which waited for: 6 -> 7; matrix products, arithmetic and copies ran while one was open for 5% -> 0% of each run, Pallas kernels for 0% -> 29%
where the time goes in v1:
time: 57.7 us; the launch traced here: 56.8 us
  Pallas kernels  26.7 us (46%)
  waiting for transfers between devices  16.3 us (28%)
  starting transfers between devices  12.8 us (22%)
  between operations  0.98 us (2%)
    pallas_call x11, Pallas kernels, call(): pl.pallas_call(body, out_shape=outs, in_specs=ins, out_specs=out_specs, s...  26.7 us
    ppermute x6, waiting for transfers between devices, partner(): return lax.ppermute(value, 'tile', pairs)  11.1 us
    ppermute x5, starting transfers between devices, moved(): lax.ppermute(value, 'tile', [(i, (i + steps) % count) for i in range(coun...  7.9 us
    ppermute x5, waiting for transfers between devices, moved(): lax.ppermute(value, 'tile', [(i, (i + steps) % count) for i in range(coun...  5.15 us
    ppermute x6, starting transfers between devices, partner(): return lax.ppermute(value, 'tile', pairs)  4.88 us
  transfers between devices with their start and end apart: 11, of which 7 were waited for; matrix products, arithmetic and copies ran while one was open for 0% of the time, Pallas kernels for 29%

profile of v1, /device:TPU:16, one launch (start us, length us, event | category | flops | bytes accessed | tf_op | source)
XLA Modules:
  0.0 56.8 jit_solution(4333692613270395077)
XLA Ops:
  0.6 1.0 %edge_rows.1 = (f32[5,1024]{1,0:T(8,128)S(1)}, f32[7,1024]{1,0:T(8,128)S(1)}, f32[1,1024]{1,0:T(1,128)S(1)}) custom-call(f32[256,1024]{1,0:T(8,128)} %s.1, f32[256,1024]{1,0:T(8,128)} %x.1, f32[256,1024]{1,0:T(8,128)} %y.1, f32[256,1024]{1,0:T(8,128)} %c.1), custom_call_target="tpu_custom_call" | custom-call | tf_op jit(solution)/shard_map/edge_rows/pallas_call | solution.py:367
  1.6 0.1 collective-permute-start.1
  1.7 0.0 copy-start
  1.7 7.6 %collective-permute-start = (f32[5,1024]{1,0:T(8,128)S(1)}, f32[5,1024]{1,0:T(8,128)S(1)}, u32[]{:S(2)}, u32[]{:S(2)}) collective-permute-start(f32[5,1024]{1,0:T(8,128)S(1)} %get-tuple-element.52), channel_id=1, source_target_pairs={{0,63},{1,0},{2,1},{3,2},{4,3},{5,4},{6,5},{7,6},{8,7},{9,8},{10,9... | collective-permute-start | bytes 61448 | tf_op jit(solution)/shard_map/ppermute | solution.py:318
  9.3 5.0 %first_step.1 = (f32[256,1024]{1,0:T(8,128)S(1)}, f32[256,1024]{1,0:T(8,128)S(1)}, f32[256,1024]{1,0:T(8,128)S(1)}, bf16[256,1024]{1,0:T(8,128)(2,1)S(1)}, f32[2...) custom-call(f32[256,1024]{1,0:T(8,128)} %s.1, ...), custom_call_target="tpu_custom_call" | custom-call | flops 5242880 | bytes 6291456 | tf_op jit(solution)/shard_map/first_step/pallas_call | solution.py:367
  14.3 0.0 collective-permute-done.refs_1_
  14.3 0.0 collective-permute-done.1.refs_2_
  14.3 6.0 %smooth_all.1 = (f32[256,1024]{1,0:T(8,128)S(1)}, f32[256,1024]{1,0:T(8,128)S(1)}, f32[8,1024]{1,0:T(8,128)S(1)}, f32[8,1024]{1,0:T(8,128)S(1)}, f32[3,1024]{1,0:T(4,128)S(1)}, /*index=5*/f32[1,1024]{1,0:T(1,128)S(1)}) custom-call(s32[1,4]{1,0:T(1,128)S(1)} %copy-done, f32[5,1024]{1,0:T(8,128)S(1)} %collective-permute-done.refs_1_, ...), custom_call_target="tpu_custom_call" | custom-call | flops 4831838208 | bytes 2097152 | tf_op jit(solution)/shard_map/smooth_all/pallas_call | solution.py:367
  20.3 0.1 collective-permute-start.2
  20.5 1.1 %second_step.1 = (f32[256,1024]{1,0:T(8,128)S(1)}, f32[256,1024]{1,0:T(8,128)S(1)}, f32[256,1024]{1,0:T(8,128)S(1)}, bf16[256,1024]{1,0:T(8,128)(2,1)S(1)}, f32[8,1024]{1,0:T(8,128)S(1)}) custom-call(f32[256,1024]{1,0:T(8,128)S(1)} %get-tuple-element.60.refs_11_.refs_0_, f32[8,1024]{1,0:T(8,128)S(1)} %get-tuple-element.64.refs_1_.refs_2_, ...), custom_call_target="tpu_custom_call" | custom-call | flops 5242880 | bytes 2097152 | tf_op jit(solution)/shard_map/second_step/pallas_call | solution.py:367
  21.6 5.1 %collective-permute-done.2.refs_0_ = f32[1,1024]{1,0:T(1,128)S(1)} collective-permute-done((f32[1,1024]{1,0:T(1,128)S(1)}, f32[1,1024]{1,0:T(1,128)S(1)}, u32[]{:S(2)}, u32[]{:S(2)}) %collective-permute-start.2) | collective-permute-done | bytes 4128 | tf_op jit(solution)/shard_map/ppermute | solution.py:318
  26.8 0.1 second_edge.1
  26.9 0.3 collective-permute-start.3
  27.2 2.7 %start_sent.1 = (bf16[4,256,256]{2,1,0:T(8,128)(2,1)S(1)}, bf16[2,256,256]{2,1,0:T(8,128)(2,1)S(1)}) custom-call(s32[1,4]{1,0:T(1,128)S(1)} %copy-done, f32[256,1024]{1,0:T(8,128)S(1)} %get-tuple-element.71.refs_1_.x_in, f32[256,1024]{1,0:T(8,128)S(1)} %get-tuple-element.72.refs_2_.y_in, bf16[256,1024]{1,0:T(8,128)(2,1)S(1)} %get-tuple-element.73.refs_3_, ...), custom_call_target="tpu_custom_call" | custom-call | flops 1610612736 | bytes 262144 | tf_op jit(solution)/shard_map/start_sent/pallas_call | solution.py:367
  29.9 1.7 %collective-permute-done.3 = f32[1,128]{1,0:T(1,128)S(1)} collective-permute-done((f32[1,128]{1,0:T(1,128)S(1)}, f32[1,128]{1,0:T(1,128)S(1)}, u32[]{:S(2)}, u32[]{:S(2)}) %collective-permute-start.3) | collective-permute-done | bytes 544 | tf_op jit(solution)/shard_map/ppermute | solution.py:386
  31.6 2.2 %finish_sent.1 = (f32[2,2,256,256]{3,2,1,0:T(8,128)S(1)}, bf16[2,256,256]{2,1,0:T(8,128)(2,1)S(1)}, bf16[2,256,256]{2,1,0:T(8,128)(2,1)S(1)}) custom-call(bf16[256,256]{1,0:T(8,128)(2,1)S(1)} %get-tuple-element.50.refs_7_.refs_5_.sm, bf16[256,256]{1,0:T(8,128)(2,1)S(1)} %get-tuple-element.51.refs_8_.refs_6_.sm_t, ...), custom_call_target="tpu_custom_call" | custom-call | flops 1610612736 | bytes 262144 | tf_op jit(solution)/shard_map/finish_sent/pallas_call | solution.py:367
  33.8 0.1 collective-permute-start.6
  33.9 0.1 collective-permute-start.7
  34.0 1.8 %collective-permute-start.4 = (f32[1,128]{1,0:T(1,128)S(1)}, f32[1,128]{1,0:T(1,128)S(1)}, u32[]{:S(2)}, u32[]{:S(2)}) collective-permute-start(f32[1,128]{1,0:T(1,128)S(1)} %add.15), channel_id=1, source_target_pairs={{0,2},{1,3},{2,0},{3,1},{4,6},{5,7},{6,4},{7,5},{8,10},{9,11},{10,... | collective-permute-start | bytes 1544 | tf_op jit(solution)/shard_map/ppermute | solution.py:386
  35.8 4.1 %collective-permute-done.4 = f32[1,128]{1,0:T(1,128)S(1)} collective-permute-done((f32[1,128]{1,0:T(1,128)S(1)}, f32[1,128]{1,0:T(1,128)S(1)}, u32[]{:S(2)}, u32[]{:S(2)}) %collective-permute-start.4) | collective-permute-done | bytes 544 | tf_op jit(solution)/shard_map/ppermute | solution.py:386
  39.9 0.0 collective-permute-start.5
  39.9 2.6 %start_own.1 = (bf16[2,256,256]{2,1,0:T(8,128)(2,1)S(1)}, bf16[1,256,256]{2,1,0:T(8,128)(2,1)S(1)}) custom-call(s32[1,4]{1,0:T(1,128)S(1)} %copy-done, f32[256,1024]{1,0:T(8,128)S(1)} %get-tuple-element.71.refs_1_.x_in, f32[256,1024]{1,0:T(8,128)S(1)} %get-tuple-element.72.refs_2_.y_in, bf16[256,1024]{1,0:T(8,128)(2,1)S(1)} %get-tuple-element.73.refs_3_, ...), custom_call_target="tpu_custom_call" | custom-call | flops 805306368 | bytes 262144 | tf_op jit(solution)/shard_map/start_own/pallas_call | solution.py:367
  42.5 1.0 %collective-permute-done.5 = f32[1,128]{1,0:T(1,128)S(1)} collective-permute-done((f32[1,128]{1,0:T(1,128)S(1)}, f32[1,128]{1,0:T(1,128)S(1)}, u32[]{:S(2)}, u32[]{:S(2)}) %collective-permute-start.5) | collective-permute-done | bytes 544 | tf_op jit(solution)/shard_map/ppermute | solution.py:386
  43.4 4.3 %finish_own.1 = (f32[256,1024]{1,0:T(8,128)}, f32[256,1024]{1,0:T(8,128)}, f32[256,1024]{1,0:T(8,128)}, f32[3,2,256,256]{3,2,1,0:T(8,128)}) custom-call(s32[1,4]{1,0:T(1,128)S(1)} %copy-done, bf16[256,256]{1,0:T(8,128)(2,1)S(1)} %get-tuple-element.50.refs_7_.refs_5_.sm, bf16[256,256]{1,0:T(8,128)(2,1)S(1)} %get-tuple-element.51.refs_8_.refs_6_.sm_t, ...), custom_call_target="tpu_custom_call" | custom-call | flops 805306368 | bytes 3145728 | tf_op jit(solution)/shard_map/finish_own/pallas_call | solution.py:367
  47.8 0.4 collective-permute-done.8
  48.2 0.0 collective-permute-start.9
  48.2 1.1 %collective-permute-done.9 = f32[1,128]{1,0:T(1,128)S(1)} collective-permute-done((f32[1,128]{1,0:T(1,128)S(1)}, f32[1,128]{1,0:T(1,128)S(1)}, u32[]{:S(2)}, u32[]{:S(2)}) %collective-permute-start.9) | collective-permute-done | bytes 544 | tf_op jit(solution)/shard_map/ppermute | solution.py:386
  49.3 2.8 %collective-permute-start.10 = (f32[1,128]{1,0:T(1,128)S(1)}, f32[1,128]{1,0:T(1,128)S(1)}, u32[]{:S(2)}, u32[]{:S(2)}) collective-permute-start(f32[1,128]{1,0:T(1,128)S(1)} %add.19.mine), channel_id=1, source_target_pairs={{0,12},{1,13},{2,14},{3,15},{4,8},{5,9},{6,10},{7,11},{8,4},{9,5},... | collective-permute-start | bytes 1544 | tf_op jit(solution)/shard_map/ppermute | solution.py:386
  52.1 2.8 %collective-permute-done.10.received = f32[1,128]{1,0:T(1,128)S(1)} collective-permute-done((f32[1,128]{1,0:T(1,128)S(1)}, f32[1,128]{1,0:T(1,128)S(1)}, u32[]{:S(2)}, u32[]{:S(2)}) %collective-permute-start.10) | collective-permute-done | bytes 544 | tf_op jit(solution)/shard_map/ppermute | solution.py:386
  55.0 0.6 %add_shares.1 = f32[2]{0:T(128)} custom-call(f32[1,128]{1,0:T(1,128)S(1)} %add.19.mine, f32[1,128]{1,0:T(1,128)S(1)} %collective-permute-done.10.received), custom_call_target="tpu_custom_call" | custom-call | tf_op jit(solution)/shard_map/add_shares/pallas_call | solution.py:367
  55.6 0.0 collective-permute-done.7.far
  55.6 1.0 %settle_resident.1 = f32[3,2,256,256]{3,2,1,0:T(8,128)} custom-call(bf16[2,256,256]{2,1,0:T(8,128)(2,1)S(1)} %collective-permute-done.6.near, bf16[2,256,256]{2,1,0:T(8,128)(2,1)S(1)} %collective-permute-done.7.far, f32[3,2,256,256]{3,2,1,0:T(8,128)} %get-tuple-element.93.held_resident), custom_call_target="tpu_custom_call", output_to_operand_aliasing={{}: (2, {})} | custom-call | bytes 1572864 | tf_op jit(solution)/shard_map/settle_resident/pallas_call | solution.py:367
  (11 shorter events, 0.0 us)
Async XLA Ops:
  1.6 12.7 %collective-permute-start.1 = (f32[7,1024]{1,0:T(8,128)S(1)}, f32[7,1024]{1,0:T(8,128)S(1)}, u32[]{:S(2)}, u32[]{:S(2)}) collective-permute-start(f32[7,1024]{1,0:T(8,128)S(1)} %get-tuple-element.53), channel_id=1, source_target_pairs={{0,1},{1,2},{2,3},{3,4},{4,5},{5,6},{6,7},{7,8},{8,9},{9,10},{10,1... | collective-permute-start | bytes 86024 | tf_op jit(solution)/shard_map/ppermute | solution.py:318
  1.7 12.6 %copy-start = (s32[1,4]{1,0:T(1,128)S(1)}, s32[1,4]{1,0:T(1,128)}, u32[]{:S(2)}) copy-start(s32[1,4]{1,0:T(1,128)} %plan.1) | copy-start | bytes 52
  1.7 12.6 %collective-permute-start = (f32[5,1024]{1,0:T(8,128)S(1)}, f32[5,1024]{1,0:T(8,128)S(1)}, u32[]{:S(2)}, u32[]{:S(2)}) collective-permute-start(f32[5,1024]{1,0:T(8,128)S(1)} %get-tuple-element.52), channel_id=1, source_target_pairs={{0,63},{1,0},{2,1},{3,2},{4,3},{5,4},{6,5},{7,6},{8,7},{9,8},{10,9... | collective-permute-start | bytes 61448 | tf_op jit(solution)/shard_map/ppermute | solution.py:318
  20.3 6.4 %collective-permute-start.2 = (f32[1,1024]{1,0:T(1,128)S(1)}, f32[1,1024]{1,0:T(1,128)S(1)}, u32[]{:S(2)}, u32[]{:S(2)}) collective-permute-start(f32[1,1024]{1,0:T(1,128)S(1)} %get-tuple-element.62), channel_id=1, source_target_pairs={{0,1},{1,2},{2,3},{3,4},{4,5},{5,6},{6,7},{7,8},{8,9},{9,10},{10,1... | collective-permute-start | bytes 12296 | tf_op jit(solution)/shard_map/ppermute | solution.py:318
  26.9 4.7 %collective-permute-start.3 = (f32[1,128]{1,0:T(1,128)S(1)}, f32[1,128]{1,0:T(1,128)S(1)}, u32[]{:S(2)}, u32[]{:S(2)}) collective-permute-start(f32[1,128]{1,0:T(1,128)S(1)} %get-tuple-element.70), channel_id=1, source_target_pairs={{0,4},{1,5},{2,6},{3,7},{4,0},{5,1},{6,2},{7,3},{8,12},{9,13},{10,... | collective-permute-start | bytes 1544 | tf_op jit(solution)/shard_map/ppermute | solution.py:386
  33.8 21.8 %collective-permute-start.6 = (bf16[2,256,256]{2,1,0:T(8,128)(2,1)S(1)}, bf16[2,256,256]{2,1,0:T(8,128)(2,1)S(1)}, u32[]{:S(2)}, u32[]{:S(2)}) collective-permute-start(bf16[2,256,256]{2,1,0:T(8,128)(2,1)S(1)} %get-tuple-element.89), channel_id=1, source_target_pairs={{0,1},{1,2},{2,3},{3,4},{4,5},{5,6},{6,7},{7,8},{8,9},{9,10},{10,1... | collective-permute-start | bytes 786440 | tf_op jit(solution)/shard_map/ppermute | solution.py:318
  33.9 21.7 %collective-permute-start.7 = (bf16[2,256,256]{2,1,0:T(8,128)(2,1)S(1)}, bf16[2,256,256]{2,1,0:T(8,128)(2,1)S(1)}, u32[]{:S(2)}, u32[]{:S(2)}) collective-permute-start(bf16[2,256,256]{2,1,0:T(8,128)(2,1)S(1)} %get-tuple-element.90), channel_id=1, source_target_pairs={{0,2},{1,3},{2,4},{3,5},{4,6},{5,7},{6,8},{7,9},{8,10},{9,11},{10,... | collective-permute-start | bytes 786440 | tf_op jit(solution)/shard_map/ppermute | solution.py:318
  34.0 5.9 %collective-permute-start.4 = (f32[1,128]{1,0:T(1,128)S(1)}, f32[1,128]{1,0:T(1,128)S(1)}, u32[]{:S(2)}, u32[]{:S(2)}) collective-permute-start(f32[1,128]{1,0:T(1,128)S(1)} %add.15), channel_id=1, source_target_pairs={{0,2},{1,3},{2,0},{3,1},{4,6},{5,7},{6,4},{7,5},{8,10},{9,11},{10,... | collective-permute-start | bytes 1544 | tf_op jit(solution)/shard_map/ppermute | solution.py:386
  39.9 3.5 %collective-permute-start.5 = (f32[1,128]{1,0:T(1,128)S(1)}, f32[1,128]{1,0:T(1,128)S(1)}, u32[]{:S(2)}, u32[]{:S(2)}) collective-permute-start(f32[1,128]{1,0:T(1,128)S(1)} %add.16), channel_id=1, source_target_pairs={{0,16},{1,17},{2,18},{3,19},{4,20},{5,21},{6,22},{7,23},{8,24},{9,... | collective-permute-start | bytes 1544 | tf_op jit(solution)/shard_map/ppermute | solution.py:386
  43.4 4.8 %collective-permute-start.8 = (f32[1,128]{1,0:T(1,128)S(1)}, f32[1,128]{1,0:T(1,128)S(1)}, u32[]{:S(2)}, u32[]{:S(2)}) collective-permute-start(f32[1,128]{1,0:T(1,128)S(1)} %add.17), channel_id=1, source_target_pairs={{0,48},{1,49},{2,50},{3,51},{4,52},{5,53},{6,54},{7,55},{8,56},{9,... | collective-permute-start | bytes 1544 | tf_op jit(solution)/shard_map/ppermute | solution.py:386
  48.2 1.1 %collective-permute-start.9 = (f32[1,128]{1,0:T(1,128)S(1)}, f32[1,128]{1,0:T(1,128)S(1)}, u32[]{:S(2)}, u32[]{:S(2)}) collective-permute-start(f32[1,128]{1,0:T(1,128)S(1)} %add.18), channel_id=1, source_target_pairs={{0,1},{1,0},{2,3},{3,2},{4,5},{5,4},{6,7},{7,6},{8,9},{9,8},{10,11... | collective-permute-start | bytes 1544 | tf_op jit(solution)/shard_map/ppermute | solution.py:386
  49.3 5.7 %collective-permute-start.10 = (f32[1,128]{1,0:T(1,128)S(1)}, f32[1,128]{1,0:T(1,128)S(1)}, u32[]{:S(2)}, u32[]{:S(2)}) collective-permute-start(f32[1,128]{1,0:T(1,128)S(1)} %add.19.mine), channel_id=1, source_target_pairs={{0,12},{1,13},{2,14},{3,15},{4,8},{5,9},{6,10},{7,11},{8,4},{9,5},... | collective-permute-start | bytes 1544 | tf_op jit(solution)/shard_map/ppermute | solution.py:386

commit v2 on v1

v2 whole, which is shorter than its diff:
```python
import jax
import jax.numpy as jnp
from jax import lax
from jax.experimental import pallas as pl
from jax.experimental.pallas import tpu as pltpu
from jax.sharding import PartitionSpec as P

SUB = 12
PIECES = (6, 6)
EDGE = 8
PACK = 16
BAND = 32
LOAD = 64
GRANT = 16 * 2**20
F32 = jnp.float32
BF16 = jnp.bfloat16
VMEM = pl.BlockSpec(memory_space=pltpu.VMEM)
SMEM = pl.BlockSpec(memory_space=pltpu.SMEM)
HBM = pl.BlockSpec(memory_space=pltpu.HBM)


def shifted_left(rows, half):
    cols = rows.shape[1]
    ids = lax.broadcasted_iota(jnp.int32, rows.shape, 1) % half
    return jnp.where(ids == half - 1, 0.0, pltpu.roll(rows, cols - 1, 1))


def shifted_right(rows, half):
    ids = lax.broadcasted_iota(jnp.int32, rows.shape, 1) % half
    return jnp.where(ids == 0, 0.0, pltpu.roll(rows, 1, 1))


def drag_of(rough, level, depth):
    return (rough / jnp.maximum(level + depth, 1.0)).astype(BF16)


def code_column(plan, code, side):
    column = 0
    for k in range(plan.shape[1]):
        column = column + jnp.where(plan[0, k] == code, k * side, 0)
    return pl.multiple_of(column, side)


def of_code(code, codes, rows, side):
    block = jnp.zeros((rows.shape[0], side), rows.dtype)
    for k in range(codes.shape[1]):
        block = jnp.where(codes[0:1, k:k + 1] == code, rows[:, k * side:(k + 1) * side], block)
    return block


def put_blocks(plan, x, y, drag, held, drags):
    side = held.shape[-1]
    for k in range(plan.shape[1]):
        code, span = plan[0, k], pl.ds(k * side, side)
        held[code, 0] = x[:, span].astype(BF16)
        held[code, 1] = y[:, span].astype(BF16)
        drags[code] = drag[:, span]


def advance(half, level, ahead, flow_x, flow_y, celerity, above_x):
    rows = level.shape[0]
    row_ids = lax.broadcasted_iota(jnp.int32, level.shape, 0)
    below = jnp.where(row_ids == rows - 1, ahead, pltpu.roll(level, rows - 1, 0))
    new_x = flow_x - celerity * (below - level)
    new_y = flow_y - celerity * (shifted_left(level, half) - level)
    behind_x = jnp.where(row_ids == 0, above_x, pltpu.roll(new_x, 1, 0))
    new_level = level - (new_x - behind_x) - (new_y - shifted_right(new_y, half))
    return new_x, new_y, new_level


def edge_rows(s, x, y, c, up, down, first, heads, tails, sems):
    rows = s.shape[0]
    copies = []
    for j, array in enumerate((s, x, y, c)):
        copies.append(pltpu.make_async_copy(array.at[pl.ds(0, EDGE)], heads.at[j], sems.at[2 * j]))
        copies.append(pltpu.make_async_copy(array.at[pl.ds(rows - EDGE, EDGE)], tails.at[j], sems.at[2 * j + 1]))
    for copy in copies:
        copy.start()
    for copy in copies:
        copy.wait()
    up[0:2] = heads[0, 0:2]
    for j in range(1, 4):
        up[j + 1:j + 2] = heads[j, 0:1]
    down[0:2] = tails[0, EDGE - 2:]
    down[2:4] = tails[1, EDGE - 2:]
    down[4:6] = tails[3, EDGE - 2:]
    down[6:7] = tails[2, EDGE - 1:]
    first[...] = heads[0, 0:1]


def first_step(s_in, x_in, y_in, c, b, r, sm, x_out, y_out, l_out, d_out, sm_t, s, x, y, sems):
    total, cols = s.shape
    half = cols // 2
    loads = total // LOAD
    pairs = ((s_in, s), (x_in, x), (y_in, y))

    def copy(i, j):
        rows = pl.ds(i * LOAD, LOAD)
        source, target = pairs[j]
        return pltpu.make_async_copy(source.at[rows], target.at[rows], sems.at[i, j])

    for i in range(loads):
        for j in range(len(pairs)):
            copy(i, j).start()
    sm_t[...] = sm[...].T
    above = jnp.zeros((1, cols), F32)
    for j in range(len(pairs)):
        copy(0, j).wait()
    for i in range(loads):
        if i + 1 < loads:
            for j in range(len(pairs)):
                copy(i + 1, j).wait()
        for start in range(i * LOAD, (i + 1) * LOAD, BAND):
            rows = pl.ds(start, BAND)
            if start + BAND < total:
                ahead = s[pl.ds(start + BAND, 1)]
            else:
                ahead = jnp.zeros((1, cols), F32)
            new_x, new_y, level = advance(half, s[rows], ahead, x[rows], y[rows], c[rows], above)
            above = new_x[BAND - 1:]
            x_out[rows] = new_x
            y_out[rows] = new_y
            l_out[rows] = level
            d_out[rows] = drag_of(r[rows], level, b[rows])


def row_weight(shape, start, total_rows):
    ids = lax.broadcasted_iota(jnp.int32, shape, 0) + start
    return 1.0 + ids.astype(F32) * (2.0 / total_rows)


def second_step(tile_count, plan_in, l_in, l_head, l_tail, halo, x_in, y_in, c, b, r,
                x_out, y_out, l_out, held, drags, sums_out, plan, drag, plan_sem):
    total, cols = l_in.shape
    half = cols // 2
    bands = total // BAND
    position = lax.axis_index("tile")
    plan_copy = pltpu.make_async_copy(plan_in, plan, plan_sem)
    plan_copy.start()

    def level_band(i):
        start, stop = i * BAND, (i + 1) * BAND
        parts = [l_in[pl.ds(start, BAND)]]
        if i == 0:
            parts = [l_head[...], l_in[pl.ds(EDGE, BAND - EDGE)]]
        if i == bands - 1:
            parts = [l_in[pl.ds(start, BAND - EDGE)], l_tail[...]]
        return jnp.concatenate(parts, 0)

    above = jnp.zeros((1, cols), F32)
    sums = jnp.zeros((EDGE, cols), F32)
    level = level_band(0)
    for i in range(bands):
        rows = pl.ds(i * BAND, BAND)
        following = level_band(i + 1) if i + 1 < bands else halo[...]
        new_x, new_y, new_level = advance(half, level, following[0:1], x_in[rows], y_in[rows], c[rows], above)
        level = following
        above = new_x[BAND - 1:]
        x_out[rows] = new_x
        y_out[rows] = new_y
        l_out[rows] = new_level
        drag[rows] = drag_of(r[rows], new_level, b[rows])
        for j in range(BAND // EDGE):
            if i + j > 0:
                part = new_level[j * EDGE:(j + 1) * EDGE]
                weight = row_weight(part.shape, position * total + i * BAND + j * EDGE, tile_count * total)
                sums = sums + weight * (part * part)
    sums_out[...] = sums
    plan_copy.wait()
    put_blocks(plan, x_out, y_out, drag, held, drags)


def second_edge(tile_count, row_count, plan, down, halo, l_head, l2_head, sums, b_head, r_head, drags_in, head, drags, shares):
    cols = l_head.shape[1]
    half = cols // 2
    position = lax.axis_index("tile")
    total_rows = tile_count * row_count
    has_previous = jnp.where(position == 0, 0.0, 1.0)
    above_x = has_previous * (down[...] - halo[2:3] * (l_head[0:1] - halo[1:2]))
    row_ids = lax.broadcasted_iota(jnp.int32, (PACK, cols), 0)
    level = l2_head[...] + jnp.where(row_ids == 0, above_x, 0.0)
    head[...] = level
    drag, codes = drag_of(r_head[...], level, b_head[...]).astype(F32), plan[...]
    for slot in range(drags.shape[0]):
        drags[slot] = drags_in[slot + 1]
        drags[slot, 0:PACK] = of_code(slot + 1, codes, drag, drags.shape[-1]).astype(BF16)
    top = level[:EDGE]
    whole = sums[...] + row_weight(top.shape, position * row_count, total_rows) * (top * top)
    lanes = lax.broadcasted_iota(jnp.int32, (1, 128), 1)
    share = jnp.zeros((1, 128), F32)
    for scenario in range(2):
        part = whole[:, scenario * half:(scenario + 1) * half]
        share = jnp.where(lanes == 2 * position + scenario, jnp.sum(part) * (1.0 / (total_rows * half)), share)
    shares[...] = share


def soften(smooth, smooth_t, source, held, drags, repeats, put=None):
    for repeat in range(repeats):
        for slot in range(drags.shape[0]):
            for f in range(2):
                start = source if repeat == 0 else held
                mixed = jnp.dot(start[slot, f], smooth_t, preferred_element_type=F32).astype(BF16)
                full = jnp.dot(smooth, mixed, preferred_element_type=F32)
                settled = full / (1.0 + drags[slot].astype(F32) * jnp.abs(full))
                if put is None or repeat + 1 < repeats:
                    held[slot, f] = settled.astype(BF16)
                else:
                    put(slot, f, settled)


def smooth_all(tile_count, plan_in, up, down, first, c, b, r, sm, sm_t, x_in, y_in, l_in, d_in,
               x, y, l_head, l_tail, halo, x_last, held, drags, edge, low_x, plan, plan_sem):
    plan_copy = pltpu.make_async_copy(plan_in, plan, plan_sem)
    plan_copy.start()
    rows, cols = x.shape
    half = cols // 2
    side = sm.shape[0]
    position = lax.axis_index("tile")
    has_next = jnp.where(position == tile_count - 1, 0.0, 1.0)
    has_previous = jnp.where(position == 0, 0.0, 1.0)
    below = up[...] * has_next
    above = down[...] * has_previous
    tail, head = pl.ds(rows - EDGE, EDGE), pl.ds(0, EDGE)
    row_ids = lax.broadcasted_iota(jnp.int32, (EDGE, cols), 0)
    own_first = first[...]

    change = jnp.where(row_ids == EDGE - 1, c[tail] * below[0:1], 0.0)
    x_tail = x_in[tail] - change
    low_x[0:EDGE] = x_in[pl.ds(rows - PACK, EDGE)]
    low_x[EDGE:PACK] = x_tail
    low = l_in[tail] + change
    l_tail[...] = low
    above_x = above[3:4] - above[5:6] * (own_first - above[1:2])
    top = l_in[head] + jnp.where(row_ids == 0, above_x, 0.0)
    l_head[...] = top

    next_x = below[2:3] - below[4:5] * (below[1:2] - below[0:1])
    next_y = below[3:4] - below[4:5] * (shifted_left(below[0:1], half) - below[0:1])
    next_level = below[0:1] - (next_x - x_tail[EDGE - 1:]) - (next_y - shifted_right(next_y, half))
    halo[0:1] = has_next * next_level
    before_x = above[2:3] - above[4:5] * (above[1:2] - above[0:1])
    before_y = above[6:7] - above[5:6] * (shifted_left(above[1:2], half) - above[1:2])
    halo[1:2] = above[1:2] - (above_x - before_x) - (before_y - shifted_right(before_y, half))
    halo[2:3] = above[5:6]

    first_rows, last_rows = pl.ds(0, PACK), pl.ds(rows - PACK, PACK)
    first_edge, last_edge = pl.ds(0, PACK), pl.ds(PACK, PACK)
    edge[first_edge] = drag_of(r[first_rows], jnp.concatenate([top, l_in[pl.ds(EDGE, EDGE)]], 0), b[first_rows])
    edge[last_edge] = drag_of(r[last_rows], jnp.concatenate([l_in[pl.ds(rows - PACK, EDGE)], low], 0), b[last_rows])
    plan_copy.wait()
    dry = pl.ds(code_column(plan, 0, side), side)
    x[:, dry] = x_in[:, dry]
    x[last_rows, dry] = low_x[:, dry]
    y[:, dry] = y_in[:, dry]
    columns = [code_column(plan, code, side) for code in (1, 2, 3)]
    for slot, column in enumerate(columns):
        span = pl.ds(column, side)
        drags[slot] = d_in[:, span]
        drags[slot, first_rows] = edge[first_edge, span]
        drags[slot, last_rows] = edge[last_edge, span]
        held[slot, 0] = x_in[:, span].astype(BF16)
        held[slot, 0, last_rows] = low_x[:, span].astype(BF16)
        held[slot, 1] = y_in[:, span].astype(BF16)

    def put(slot, f, settled):
        (x, y)[f][:, pl.ds(columns[slot], side)] = settled

    soften(sm[...], sm_t[...], held, held, drags, SUB, put)
    x_last[...] = x[rows - 1:rows]


def start_last(repeats, sm, sm_t, held_in, drags, l_in, head, held, lev, sems):
    rest, top = pl.ds(PACK, l_in.shape[0] - PACK), pl.ds(0, PACK)
    copies = [
        pltpu.make_async_copy(l_in.at[rest], lev.at[rest], sems.at[0]),
        pltpu.make_async_copy(head.at[top], lev.at[top], sems.at[1]),
    ]
    for copy in copies:
        copy.start()
    soften(sm[...], sm_t[...], held_in.at[pl.ds(1, 3)], held, drags, repeats)
    for copy in copies:
        copy.wait()


def go_on(repeats, sm, sm_t, held_in, drags, held):
    soften(sm[...], sm_t[...], held_in, held, drags, repeats)


def finish_last(repeats, plan_in, sm, sm_t, held_in, drags, x_in, y_in, x, y, own, near, far, held, plan, plan_sem):
    plan_copy = pltpu.make_async_copy(plan_in, plan, plan_sem)
    plan_copy.start()
    side = sm.shape[0]
    columns = []

    def put(slot, f, settled):
        if not columns:
            plan_copy.wait()
            columns.extend(code_column(plan, code, side) for code in range(4))
        (x, y)[f][:, pl.ds(columns[slot + 1], side)] = settled
        if slot == 0:
            own[f] = settled
        else:
            (near, far)[slot - 1][f] = settled.astype(BF16)

    soften(sm[...], sm_t[...], held_in, held, drags, repeats, put)
    dry = pl.ds(columns[0], side)
    x[:, dry] = x_in[:, dry]
    y[:, dry] = y_in[:, dry]


def put_fluxes(x_in, y_in, own, x, y, resident, sems):
    copies = [
        pltpu.make_async_copy(source, target, sems.at[i])
        for i, (source, target) in enumerate(((x_in, x), (y_in, y), (own, resident.at[0])))
    ]
    for copy in copies:
        copy.start()
    for copy in copies:
        copy.wait()


def put_received(near, far, resident_held, resident, stage, sems):
    copies = []
    for slot, block in enumerate((near, far)):
        stage[slot] = block[...].astype(F32)
        copies.append(pltpu.make_async_copy(stage.at[slot], resident.at[slot + 1], sems.at[slot]))
        copies[-1].start()
    for copy in copies:
        copy.wait()


def add_shares(mine, received, energy):
    shares = mine[...] + received[...]
    lanes = lax.broadcasted_iota(jnp.int32, shares.shape, 1)
    for scenario in range(2):
        energy[scenario] = jnp.sum(jnp.where(lanes % 2 == scenario, shares, 0.0))


def moved(value, steps):
    count = lax.axis_size("tile")
    return lax.ppermute(value, "tile", [(i, (i + steps) % count) for i in range(count)])


def exchange_stages(count):
    deep = 8 if count >= 16 else max(count // 2, 1)
    wide = count // (2 * deep)

    def index(x, z, core):
        return (x * deep + z) * 2 + core

    def stage(rule):
        pairs = []
        for i in range(count):
            core, z, x = i % 2, (i // 2) % deep, i // (2 * deep)
            pairs.append((i, index(*rule(x, z, core))))
        return pairs

    stages = []
    if deep == 8:
        across = {0: 6, 6: 0, 2: 4, 4: 2, 1: 7, 7: 1, 3: 5, 5: 3}
        stages.append(stage(lambda x, z, core: (x, z ^ 2, core)))
        stages.append(stage(lambda x, z, core: (x, across[z], core)))
    if wide >= 2:
        stages.append(stage(lambda x, z, core: (x ^ 1, z, core)))
    if wide == 4:
        stages.append(stage(lambda x, z, core: (3 - x, z, core)))
    stages.append(stage(lambda x, z, core: (x, z, 1 - core)))
    reach = 1
    while reach < (2 if deep == 8 else deep):
        stages.append(stage(lambda x, z, core, reach=reach: (x, z ^ reach, core)))
        reach *= 2
    return stages


def on_device(surface, flux_x, flux_y, celerity, bed_depth, roughness, smoother, plan):
    rows, cols = surface.shape
    side = smoother.shape[0]
    tiles = lax.axis_size("tile")

    def arr(*shape, dtype=F32):
        return jax.ShapeDtypeStruct(shape, dtype)

    field, square = arr(rows, cols), arr(side, side, dtype=BF16)

    def call(body, name, ins, outs, out_specs, operands, scratch=(), aliases={}, flops=0, moved_bytes=0):
        return pl.pallas_call(
            body,
            out_shape=outs,
            in_specs=ins,
            out_specs=out_specs,
            scratch_shapes=scratch,
            input_output_aliases=aliases,
            compiler_params=pltpu.CompilerParams(vmem_limit_bytes=GRANT),
            cost_estimate=pl.CostEstimate(flops=flops, bytes_accessed=moved_bytes, transcendentals=0),
            name=name,
        )(*operands)

    def dots(chains, repeats):
        return chains * repeats * 4 * side**3

    def partner(value, pairs):
        return lax.ppermute(value, "tile", pairs)

    c, b, r, sm = celerity, bed_depth, roughness, smoother
    codes = plan
    surface, flux_x, flux_y, celerity, plan = [
        pltpu.with_memory_space_constraint(array, pltpu.HBM)
        for array in (surface, flux_x, flux_y, celerity, plan)
    ]
    plan_scratch = [pltpu.SMEM(plan.shape, plan.dtype), pltpu.SemaphoreType.DMA]
    held_shape, drag_shape = arr(4, 2, side, side, dtype=BF16), arr(4, side, side, dtype=BF16)
    wet_held, wet_drags = arr(3, 2, side, side, dtype=BF16), arr(3, side, side, dtype=BF16)
    up, down, first = call(
        edge_rows, "edge_rows", [HBM] * 4, (arr(5, cols), arr(7, cols), arr(1, cols)), [VMEM] * 3,
        (surface, flux_x, flux_y, celerity),
        [pltpu.VMEM((4, EDGE, cols), F32)] * 2 + [pltpu.SemaphoreType.DMA((8,))])
    up = moved(up, -1)
    down = moved(down, 1)
    x, y, lev, d, sm_t = call(
        first_step, "first_step", [HBM] * 3 + [VMEM] * 4,
        (field, field, field, arr(rows, cols, dtype=BF16), square), [VMEM] * 5,
        (surface, flux_x, flux_y, c, b, r, sm),
        [pltpu.VMEM((rows, cols), F32)] * 3 + [pltpu.SemaphoreType.DMA((rows // LOAD, 3))],
        flops=20 * rows * cols, moved_bytes=24 * rows * cols)
    held_scratch, drag_scratch = pltpu.VMEM(wet_held.shape, BF16), pltpu.VMEM(wet_drags.shape, BF16)
    x, y, l_head, l_tail, halo, x_last = call(
        lambda *refs: smooth_all(tiles, *refs), "smooth_all", [HBM] + [VMEM] * 12,
        (field, field, arr(EDGE, cols), arr(EDGE, cols), arr(3, cols), arr(1, cols)), [VMEM] * 6,
        (plan, up, down, first, c, b, r, sm, sm_t, x, y, lev, d),
        [held_scratch, drag_scratch, pltpu.VMEM((2 * PACK, cols), BF16), pltpu.VMEM((PACK, cols), F32)] + plan_scratch,
        flops=dots(6, SUB), moved_bytes=8 * rows * cols)
    down = moved(x_last, 1)
    x, y, lev, held, drags, sums = call(
        lambda *refs: second_step(tiles, *refs), "second_step", [HBM] + [VMEM] * 9,
        (field, field, field, held_shape, drag_shape, arr(EDGE, cols)), [VMEM] * 6,
        (plan, lev, l_head, l_tail, halo, x, y, c, b, r),
        plan_scratch[:1] + [pltpu.VMEM((rows, cols), BF16)] + plan_scratch[1:],
        flops=20 * rows * cols, moved_bytes=8 * rows * cols)
    head, drags, shares = call(
        lambda *refs: second_edge(tiles, rows, *refs), "second_edge", [VMEM] * 9,
        (arr(PACK, cols), wet_drags, arr(1, 128)), [VMEM] * 3,
        (codes, down, halo, l_head, lev[:PACK], sums, b[:PACK], r[:PACK], drags), flops=cols, moved_bytes=cols)

    stages = exchange_stages(tiles)
    done = 0

    def exchange(shares, beside):
        nonlocal done
        if done + 1 >= len(stages):
            return (shares,) + tuple(beside())
        met = lax.ppermute(shares, "tile", stages[done])
        done += 1
        return lax.optimization_barrier((shares + met,) + tuple(beside()))

    pair, resident_shape = arr(2, side, side, dtype=BF16), arr(3, 2, side, side)
    shares, held, level = exchange(shares, lambda: call(
        lambda *refs: start_last(PIECES[0], *refs), "start_last", [VMEM] * 6, (wet_held, field), [VMEM, HBM],
        (sm, sm_t, held, drags, lev, head), [pltpu.SemaphoreType.DMA((2,))],
        flops=dots(6, PIECES[0]), moved_bytes=rows * cols))
    for piece in PIECES[1:-1]:
        shares, held = exchange(shares, lambda: (call(
            lambda *refs: go_on(piece, *refs), "go_on", [VMEM] * 4, wet_held, VMEM, (sm, sm_t, held, drags),
            flops=dots(6, piece), moved_bytes=rows * cols),))
    shares, x, y, own, near, far = exchange(shares, lambda: call(
        lambda *refs: finish_last(PIECES[-1], *refs), "finish_last", [HBM] + [VMEM] * 6,
        (field, field, arr(2, side, side), pair, pair), [VMEM] * 5,
        (plan, sm, sm_t, held, drags, x, y), [held_scratch] + plan_scratch,
        flops=dots(6, PIECES[-1]), moved_bytes=rows * cols))
    near, far = moved(near, 1), moved(far, 2)
    shares, x, y, resident = exchange(shares, lambda: call(
        put_fluxes, "put_fluxes", [VMEM] * 3, (field, field, resident_shape), [HBM] * 3,
        (x, y, own), [pltpu.SemaphoreType.DMA((3,))], moved_bytes=16 * rows * cols))
    while done + 1 < len(stages):
        shares, = exchange(shares, tuple)
    met = lax.ppermute(shares, "tile", stages[done])
    resident = call(
        put_received, "put_received", [VMEM] * 2 + [HBM], resident_shape, HBM, (near, far, resident),
        [pltpu.VMEM((2, 2, side, side), F32), pltpu.SemaphoreType.DMA((2,))],
        aliases={2: 0}, moved_bytes=24 * side * side)
    energy = call(add_shares, "add_shares", [VMEM] * 2, arr(2), SMEM, (shares, met))
    return level, x, y, resident, energy


def solution(mesh):
    cut = P(("ens", "tile"), None)
    return jax.shard_map(
        on_device,
        mesh=mesh,
        in_specs=(cut,) * 6 + (P(), cut),
        out_specs=(cut, cut, cut, P(("ens", "tile"), None, None, None), P("ens")),
        check_vma=False,
    )
```

time: 57.7 us -> 52 us (0.901)
  the two profiles are of different devices: /device:TPU:16 before, /device:TPU:1 now
where the time goes in v2:
time: 52 us; the launch traced here: 51.8 us
  Pallas kernels  22 us (42%)
  starting transfers between devices  17.9 us (34%)
  waiting for transfers between devices  11 us (21%)
  between operations  0.97 us (2%)
    pallas_call x10, Pallas kernels, call(): pl.pallas_call(body, out_shape=outs, in_specs=ins, out_specs=out_specs, s...  22 us
    ppermute x5, starting transfers between devices, moved(): lax.ppermute(value, 'tile', [(i, (i + steps) % count) for i in range(coun...  12 us
    ppermute x5, waiting for transfers between devices, exchange(): met = lax.ppermute(shares, 'tile', stages[done])  5.89 us
    ppermute x5, waiting for transfers between devices, moved(): lax.ppermute(value, 'tile', [(i, (i + steps) % count) for i in range(coun...  4.15 us
    ppermute x5, starting transfers between devices, exchange(): met = lax.ppermute(shares, 'tile', stages[done])  3.71 us
    ppermute x1, starting transfers between devices, on_device(): met = lax.ppermute(shares, 'tile', stages[done])  2.13 us
  transfers between devices with their start and end apart: 11, of which 7 were waited for; matrix products, arithmetic and copies ran while one was open for 0% of the time, Pallas kernels for 26%

profile of v2, /device:TPU:1, one launch (start us, length us, event | category | flops | bytes accessed | tf_op | source)
XLA Modules:
  0.0 51.8 jit_solution(548173465004827750)
XLA Ops:
  0.7 1.1 %edge_rows.1 = (f32[5,1024]{1,0:T(8,128)S(1)}, f32[7,1024]{1,0:T(8,128)S(1)}, f32[1,1024]{1,0:T(1,128)S(1)}) custom-call(f32[256,1024]{1,0:T(8,128)} %s_in.1, f32[256,1024]{1,0:T(8,128)} %x_in.1, f32[256,1024]{1,0:T(8,128)} %y_in.1, f32[256,1024]{1,0:T(8,128)} %refs_7_.3), custom_call_target="tpu_custom_call" | custom-call | tf_op jit(solution)/shard_map/edge_rows/pallas_call | solution.py:386
  1.8 3.1 %collective-permute-start.1 = (f32[7,1024]{1,0:T(8,128)S(1)}, f32[7,1024]{1,0:T(8,128)S(1)}, u32[]{:S(2)}, u32[]{:S(2)}) collective-permute-start(f32[7,1024]{1,0:T(8,128)S(1)} %get-tuple-element.52), channel_id=1, source_target_pairs={{0,1},{1,2},{2,3},{3,4},{4,5},{5,6},{6,7},{7,8},{8,9},{9,10},{10,1... | collective-permute-start | bytes 86024 | tf_op jit(solution)/shard_map/ppermute | solution.py:341
  4.9 0.3 collective-permute-start
  5.2 2.6 %first_step.1 = (f32[256,1024]{1,0:T(8,128)S(1)}, f32[256,1024]{1,0:T(8,128)S(1)}, f32[256,1024]{1,0:T(8,128)S(1)}, bf16[256,1024]{1,0:T(8,128)(2,1)S(1)}, bf16[256,256]{1,0:T(8,128)(2,1)S(1)}) custom-call(f32[256,1024]{1,0:T(8,128)} %s_in.1, f32[256,1024]{1,0:T(8,128)} %x_in.1, f32[256,1024]{1,0:T(8,128)} %y_in.1, f32[256,1024]{1,0:T(8,128)S(1)} %copy-done, ...), custom_call_target="tpu_custom_call" | custom-call | flops 5242880 | bytes 6291456 | tf_op jit(solution)/shard_map/first_step/pallas_call | solution.py:386
  7.8 0.4 collective-permute-done.refs_1_
  8.2 0.0 collective-permute-done.1.refs_2_
  8.2 6.0 %smooth_all.1 = (f32[256,1024]{1,0:T(8,128)S(1)}, f32[256,1024]{1,0:T(8,128)S(1)}, f32[8,1024]{1,0:T(8,128)S(1)}, f32[8,1024]{1,0:T(8,128)S(1)}, f32[3,1024]{1,0:T(4,128)S(1)}, /*index=5*/f32[1,1024]{1,0:T(1,128)S(1)}) custom-call(s32[1,4]{1,0:T(1,128)} %refs_0_.9, f32[5,1024]{1,0:T(8,128)S(1)} %collective-permute-done.refs_1_, ...), custom_call_target="tpu_custom_call" | custom-call | flops 4831838208 | bytes 2097152 | tf_op jit(solution)/shard_map/smooth_all/pallas_call | solution.py:386
  14.3 1.1 %collective-permute-start.2 = (f32[1,1024]{1,0:T(1,128)S(1)}, f32[1,1024]{1,0:T(1,128)S(1)}, u32[]{:S(2)}, u32[]{:S(2)}) collective-permute-start(f32[1,1024]{1,0:T(1,128)S(1)} %get-tuple-element.59), channel_id=1, source_target_pairs={{0,1},{1,2},{2,3},{3,4},{4,5},{5,6},{6,7},{7,8},{8,9},{9,10},{10,1... | collective-permute-start | bytes 12296 | tf_op jit(solution)/shard_map/ppermute | solution.py:341
  15.4 0.0 copy-start.4
  15.4 2.0 %second_step.1 = (f32[256,1024]{1,0:T(8,128)S(1)}, f32[256,1024]{1,0:T(8,128)S(1)}, f32[256,1024]{1,0:T(8,128)S(1)}, bf16[4,2,256,256]{3,2,1,0:T(8,128)(2,1)S(1)...) custom-call(s32[1,4]{1,0:T(1,128)} %refs_0_.9, f32[256,1024]{1,0:T(8,128)S(1)} %get-tuple-element.57.refs_11_.refs_1_, ...), custom_call_target="tpu_custom_call" | custom-call | flops 5242880 | bytes 2097152 | tf_op jit(solution)/shard_map/second_step/pallas_call | solution.py:386
  17.4 3.0 %collective-permute-done.2.refs_1_ = f32[1,1024]{1,0:T(1,128)S(1)} collective-permute-done((f32[1,1024]{1,0:T(1,128)S(1)}, f32[1,1024]{1,0:T(1,128)S(1)}, u32[]{:S(2)}, u32[]{:S(2)}) %collective-permute-start.2) | collective-permute-done | bytes 4128 | tf_op jit(solution)/shard_map/ppermute | solution.py:341
  20.4 0.1 second_edge.1
  20.6 0.3 collective-permute-start.3
  20.9 3.7 %start_last.1 = (bf16[3,2,256,256]{3,2,1,0:T(8,128)(2,1)S(1)}, f32[256,1024]{1,0:T(8,128)}) custom-call(bf16[256,256]{1,0:T(8,128)(2,1)S(1)} %copy-done.3, bf16[256,256]{1,0:T(8,128)(2,1)S(1)} %get-tuple-element.54.refs_8_.refs_1_.refs_2_, bf16[4,2,256,256]{3,2,1,0:T(8,128)(2,1)S(1)} %get-tuple-element.69.refs_2_, ...), custom_call_target="tpu_custom_call" | custom-call | flops 2415919104 | bytes 262144 | tf_op jit(solution)/shard_map/start_last/pallas_call | solution.py:386
  24.5 0.0 collective-permute-done.3
  24.6 3.4 %collective-permute-start.4 = (f32[1,128]{1,0:T(1,128)S(1)}, f32[1,128]{1,0:T(1,128)S(1)}, u32[]{:S(2)}, u32[]{:S(2)}) collective-permute-start(f32[1,128]{1,0:T(1,128)S(1)} %add.15), channel_id=1, source_target_pairs={{0,12},{1,13},{2,14},{3,15},{4,8},{5,9},{6,10},{7,11},{8,4},{9,5},... | collective-permute-start | bytes 1544 | tf_op jit(solution)/shard_map/ppermute | solution.py:451
  27.9 3.3 %finish_last.1 = (f32[256,1024]{1,0:T(8,128)S(1)}, f32[256,1024]{1,0:T(8,128)S(1)}, f32[2,256,256]{2,1,0:T(8,128)S(1)}, bf16[2,256,256]{2,1,0:T(8,128)(2,1)S(1)}, bf16[2,256,256]{2,1,0:T(8,128)(2,1)S(1)}) custom-call(s32[1,4]{1,0:T(1,128)} %refs_0_.9, bf16[256,256]{1,0:T(8,128)(2,1)S(1)} %copy-done.3, ...), custom_call_target="tpu_custom_call" | custom-call | flops 2415919104 | bytes 262144 | tf_op jit(solution)/shard_map/finish_last/pallas_call | solution.py:386
  31.3 2.7 %collective-permute-start.6 = (bf16[2,256,256]{2,1,0:T(8,128)(2,1)S(1)}, bf16[2,256,256]{2,1,0:T(8,128)(2,1)S(1)}, u32[]{:S(2)}, u32[]{:S(2)}) collective-permute-start(bf16[2,256,256]{2,1,0:T(8,128)(2,1)S(1)} %get-tuple-element.93), channel_id=1, source_target_pairs={{0,1},{1,2},{2,3},{3,4},{4,5},{5,6},{6,7},{7,8},{8,9},{9,10},{10,1... | collective-permute-start | bytes 786440 | tf_op jit(solution)/shard_map/ppermute | solution.py:341
  34.0 4.8 %collective-permute-start.7 = (bf16[2,256,256]{2,1,0:T(8,128)(2,1)S(1)}, bf16[2,256,256]{2,1,0:T(8,128)(2,1)S(1)}, u32[]{:S(2)}, u32[]{:S(2)}) collective-permute-start(bf16[2,256,256]{2,1,0:T(8,128)(2,1)S(1)} %get-tuple-element.94), channel_id=1, source_target_pairs={{0,2},{1,3},{2,4},{3,5},{4,6},{5,7},{6,8},{7,9},{8,10},{9,11},{10,... | collective-permute-start | bytes 786440 | tf_op jit(solution)/shard_map/ppermute | solution.py:341
  38.8 0.0 collective-permute-start.5
  38.8 1.5 %put_fluxes.1 = (f32[256,1024]{1,0:T(8,128)}, f32[256,1024]{1,0:T(8,128)}, f32[3,2,256,256]{3,2,1,0:T(8,128)}) custom-call(f32[256,1024]{1,0:T(8,128)S(1)} %get-tuple-element.85.x_in, f32[256,1024]{1,0:T(8,128)S(1)} %get-tuple-element.86.y_in, f32[2,256,256]{2,1,0:T(8,128)S(1)} %get-tuple-element.87.own), custom_call_target="tpu_custom_call" | custom-call | bytes 4194304 | tf_op jit(solution)/shard_map/put_fluxes/pallas_call | solution.py:386
  40.3 0.9 %collective-permute-done.5 = f32[1,128]{1,0:T(1,128)S(1)} collective-permute-done((f32[1,128]{1,0:T(1,128)S(1)}, f32[1,128]{1,0:T(1,128)S(1)}, u32[]{:S(2)}, u32[]{:S(2)}) %collective-permute-start.5) | collective-permute-done | bytes 544 | tf_op jit(solution)/shard_map/ppermute | solution.py:451
  41.2 0.0 collective-permute-start.8
  41.2 3.9 %collective-permute-done.8 = f32[1,128]{1,0:T(1,128)S(1)} collective-permute-done((f32[1,128]{1,0:T(1,128)S(1)}, f32[1,128]{1,0:T(1,128)S(1)}, u32[]{:S(2)}, u32[]{:S(2)}) %collective-permute-start.8) | collective-permute-done | bytes 544 | tf_op jit(solution)/shard_map/ppermute | solution.py:451
  45.1 0.0 collective-permute-start.9
  45.1 1.1 %collective-permute-done.9 = f32[1,128]{1,0:T(1,128)S(1)} collective-permute-done((f32[1,128]{1,0:T(1,128)S(1)}, f32[1,128]{1,0:T(1,128)S(1)}, u32[]{:S(2)}, u32[]{:S(2)}) %collective-permute-start.9) | collective-permute-done | bytes 544 | tf_op jit(solution)/shard_map/ppermute | solution.py:451
  46.2 2.1 %collective-permute-start.10 = (f32[1,128]{1,0:T(1,128)S(1)}, f32[1,128]{1,0:T(1,128)S(1)}, u32[]{:S(2)}, u32[]{:S(2)}) collective-permute-start(f32[1,128]{1,0:T(1,128)S(1)} %add.19.mine), channel_id=1, source_target_pairs={{0,2},{1,3},{2,0},{3,1},{4,6},{5,7},{6,4},{7,5},{8,10},{9,11},{10,... | collective-permute-start | bytes 1544 | tf_op jit(solution)/shard_map/ppermute | solution.py:475
  48.3 0.9 %collective-permute-done.10.received = f32[1,128]{1,0:T(1,128)S(1)} collective-permute-done((f32[1,128]{1,0:T(1,128)S(1)}, f32[1,128]{1,0:T(1,128)S(1)}, u32[]{:S(2)}, u32[]{:S(2)}) %collective-permute-start.10) | collective-permute-done | bytes 544 | tf_op jit(solution)/shard_map/ppermute | solution.py:475
  49.2 0.6 %add_shares.1 = f32[2]{0:T(128)} custom-call(f32[1,128]{1,0:T(1,128)S(1)} %add.19.mine, f32[1,128]{1,0:T(1,128)S(1)} %collective-permute-done.10.received), custom_call_target="tpu_custom_call" | custom-call | tf_op jit(solution)/shard_map/add_shares/pallas_call | solution.py:386
  49.9 0.0 collective-permute-done.6.near
  49.9 0.8 %collective-permute-done.7.far = bf16[2,256,256]{2,1,0:T(8,128)(2,1)S(1)} collective-permute-done((bf16[2,256,256]{2,1,0:T(8,128)(2,1)S(1)}, bf16[2,256,256]{2,1,0:T(8,128)(2,1)S(1)}, u32[]{:S(2)}, u32[]{:S(2)}) %collective-permute-start.7) | collective-permute-done | bytes 262176 | tf_op jit(solution)/shard_map/ppermute | solution.py:341
  50.7 1.0 %put_received.1 = f32[3,2,256,256]{3,2,1,0:T(8,128)} custom-call(bf16[2,256,256]{2,1,0:T(8,128)(2,1)S(1)} %collective-permute-done.6.near, bf16[2,256,256]{2,1,0:T(8,128)(2,1)S(1)} %collective-permute-done.7.far, f32[3,2,256,256]{3,2,1,0:T(8,128)} %get-tuple-element.95.resident_held), custom_call_target="tpu_custom_call", output_to_operand_aliasing={{}: (2, {})} | custom-call | bytes 1572864 | tf_op jit(solution)/shard_map/put_received/pallas_call | solution.py:386
  (18 shorter events, 0.1 us)
Async XLA Ops:
  0.6 4.6 %copy-start = (f32[256,1024]{1,0:T(8,128)S(1)}, f32[256,1024]{1,0:T(8,128)}, u32[]{:S(2)}) copy-start(f32[256,1024]{1,0:T(8,128)} %refs_7_.3) | copy-start | bytes 3145732
  0.6 4.6 %copy-start.1 = (f32[256,1024]{1,0:T(8,128)S(1)}, f32[256,1024]{1,0:T(8,128)}, u32[]{:S(2)}) copy-start(f32[256,1024]{1,0:T(8,128)} %refs_8_.1) | copy-start | bytes 3145732
  0.7 4.6 %copy-start.2 = (f32[256,1024]{1,0:T(8,128)S(1)}, f32[256,1024]{1,0:T(8,128)}, u32[]{:S(2)}) copy-start(f32[256,1024]{1,0:T(8,128)} %refs_9_.1) | copy-start | bytes 3145732
  0.7 4.5 %copy-start.3 = (bf16[256,256]{1,0:T(8,128)(2,1)S(1)}, bf16[256,256]{1,0:T(8,128)(2,1)}, u32[]{:S(2)}) copy-start(bf16[256,256]{1,0:T(8,128)(2,1)} %refs_1_.1) | copy-start | bytes 393220
  1.8 6.4 %collective-permute-start.1 = (f32[7,1024]{1,0:T(8,128)S(1)}, f32[7,1024]{1,0:T(8,128)S(1)}, u32[]{:S(2)}, u32[]{:S(2)}) collective-permute-start(f32[7,1024]{1,0:T(8,128)S(1)} %get-tuple-element.52), channel_id=1, source_target_pairs={{0,1},{1,2},{2,3},{3,4},{4,5},{5,6},{6,7},{7,8},{8,9},{9,10},{10,1... | collective-permute-start | bytes 86024 | tf_op jit(solution)/shard_map/ppermute | solution.py:341
  4.9 3.3 %collective-permute-start = (f32[5,1024]{1,0:T(8,128)S(1)}, f32[5,1024]{1,0:T(8,128)S(1)}, u32[]{:S(2)}, u32[]{:S(2)}) collective-permute-start(f32[5,1024]{1,0:T(8,128)S(1)} %get-tuple-element.51), channel_id=1, source_target_pairs={{0,63},{1,0},{2,1},{3,2},{4,3},{5,4},{6,5},{7,6},{8,7},{9,8},{10,9... | collective-permute-start | bytes 61448 | tf_op jit(solution)/shard_map/ppermute | solution.py:341
  14.3 6.1 %collective-permute-start.2 = (f32[1,1024]{1,0:T(1,128)S(1)}, f32[1,1024]{1,0:T(1,128)S(1)}, u32[]{:S(2)}, u32[]{:S(2)}) collective-permute-start(f32[1,1024]{1,0:T(1,128)S(1)} %get-tuple-element.59), channel_id=1, source_target_pairs={{0,1},{1,2},{2,3},{3,4},{4,5},{5,6},{6,7},{7,8},{8,9},{9,10},{10,1... | collective-permute-start | bytes 12296 | tf_op jit(solution)/shard_map/ppermute | solution.py:341
  15.4 5.0 %copy-start.4 = (s32[1,4]{1,0:T(1,128)S(1)}, s32[1,4]{1,0:T(1,128)}, u32[]{:S(2)}) copy-start(s32[1,4]{1,0:T(1,128)} %refs_0_.9) | copy-start | bytes 52
  20.6 4.0 %collective-permute-start.3 = (f32[1,128]{1,0:T(1,128)S(1)}, f32[1,128]{1,0:T(1,128)S(1)}, u32[]{:S(2)}, u32[]{:S(2)}) collective-permute-start(f32[1,128]{1,0:T(1,128)S(1)} %get-tuple-element.68), channel_id=1, source_target_pairs={{0,4},{1,5},{2,6},{3,7},{4,0},{5,1},{6,2},{7,3},{8,12},{9,13},{10,... | collective-permute-start | bytes 1544 | tf_op jit(solution)/shard_map/ppermute | solution.py:451
  24.6 6.7 %collective-permute-start.4 = (f32[1,128]{1,0:T(1,128)S(1)}, f32[1,128]{1,0:T(1,128)S(1)}, u32[]{:S(2)}, u32[]{:S(2)}) collective-permute-start(f32[1,128]{1,0:T(1,128)S(1)} %add.15), channel_id=1, source_target_pairs={{0,12},{1,13},{2,14},{3,15},{4,8},{5,9},{6,10},{7,11},{8,4},{9,5},... | collective-permute-start | bytes 1544 | tf_op jit(solution)/shard_map/ppermute | solution.py:451
  31.3 18.6 %collective-permute-start.6 = (bf16[2,256,256]{2,1,0:T(8,128)(2,1)S(1)}, bf16[2,256,256]{2,1,0:T(8,128)(2,1)S(1)}, u32[]{:S(2)}, u32[]{:S(2)}) collective-permute-start(bf16[2,256,256]{2,1,0:T(8,128)(2,1)S(1)} %get-tuple-element.93), channel_id=1, source_target_pairs={{0,1},{1,2},{2,3},{3,4},{4,5},{5,6},{6,7},{7,8},{8,9},{9,10},{10,1... | collective-permute-start | bytes 786440 | tf_op jit(solution)/shard_map/ppermute | solution.py:341
  34.0 16.7 %collective-permute-start.7 = (bf16[2,256,256]{2,1,0:T(8,128)(2,1)S(1)}, bf16[2,256,256]{2,1,0:T(8,128)(2,1)S(1)}, u32[]{:S(2)}, u32[]{:S(2)}) collective-permute-start(bf16[2,256,256]{2,1,0:T(8,128)(2,1)S(1)} %get-tuple-element.94), channel_id=1, source_target_pairs={{0,2},{1,3},{2,4},{3,5},{4,6},{5,7},{6,8},{7,9},{8,10},{9,11},{10,... | collective-permute-start | bytes 786440 | tf_op jit(solution)/shard_map/ppermute | solution.py:341
  38.8 2.4 %collective-permute-start.5 = (f32[1,128]{1,0:T(1,128)S(1)}, f32[1,128]{1,0:T(1,128)S(1)}, u32[]{:S(2)}, u32[]{:S(2)}) collective-permute-start(f32[1,128]{1,0:T(1,128)S(1)} %add.16), channel_id=1, source_target_pairs={{0,16},{1,17},{2,18},{3,19},{4,20},{5,21},{6,22},{7,23},{8,24},{9,... | collective-permute-start | bytes 1544 | tf_op jit(solution)/shard_map/ppermute | solution.py:451
  41.2 3.9 %collective-permute-start.8 = (f32[1,128]{1,0:T(1,128)S(1)}, f32[1,128]{1,0:T(1,128)S(1)}, u32[]{:S(2)}, u32[]{:S(2)}) collective-permute-start(f32[1,128]{1,0:T(1,128)S(1)} %add.17), channel_id=1, source_target_pairs={{0,48},{1,49},{2,50},{3,51},{4,52},{5,53},{6,54},{7,55},{8,56},{9,... | collective-permute-start | bytes 1544 | tf_op jit(solution)/shard_map/ppermute | solution.py:451
  45.1 1.1 %collective-permute-start.9 = (f32[1,128]{1,0:T(1,128)S(1)}, f32[1,128]{1,0:T(1,128)S(1)}, u32[]{:S(2)}, u32[]{:S(2)}) collective-permute-start(f32[1,128]{1,0:T(1,128)S(1)} %add.18), channel_id=1, source_target_pairs={{0,1},{1,0},{2,3},{3,2},{4,5},{5,4},{6,7},{7,6},{8,9},{9,8},{10,11... | collective-permute-start | bytes 1544 | tf_op jit(solution)/shard_map/ppermute | solution.py:451
  46.2 3.1 %collective-permute-start.10 = (f32[1,128]{1,0:T(1,128)S(1)}, f32[1,128]{1,0:T(1,128)S(1)}, u32[]{:S(2)}, u32[]{:S(2)}) collective-permute-start(f32[1,128]{1,0:T(1,128)S(1)} %add.19.mine), channel_id=1, source_target_pairs={{0,2},{1,3},{2,0},{3,1},{4,6},{5,7},{6,4},{7,5},{8,10},{9,11},{10,... | collective-permute-start | bytes 1544 | tf_op jit(solution)/shard_map/ppermute | solution.py:475

commit v3 on v2

--- a/solution.py
+++ b/solution.py
@@ -6,7 +6,7 @@
 from jax.sharding import PartitionSpec as P
 
 SUB = 12
-PIECES = (6, 6)
+HALF = 6
 EDGE = 8
 PACK = 16
 BAND = 32
@@ -34,27 +34,10 @@
     return (rough / jnp.maximum(level + depth, 1.0)).astype(BF16)
 
 
-def code_column(plan, code, side):
-    column = 0
-    for k in range(plan.shape[1]):
-        column = column + jnp.where(plan[0, k] == code, k * side, 0)
-    return pl.multiple_of(column, side)
-
-
-def of_code(code, codes, rows, side):
-    block = jnp.zeros((rows.shape[0], side), rows.dtype)
-    for k in range(codes.shape[1]):
-        block = jnp.where(codes[0:1, k:k + 1] == code, rows[:, k * side:(k + 1) * side], block)
-    return block
-
-
-def put_blocks(plan, x, y, drag, held, drags):
-    side = held.shape[-1]
-    for k in range(plan.shape[1]):
-        code, span = plan[0, k], pl.ds(k * side, side)
-        held[code, 0] = x[:, span].astype(BF16)
-        held[code, 1] = y[:, span].astype(BF16)
-        drags[code] = drag[:, span]
+def code_column(codes, code, side):
+    place = lax.broadcasted_iota(jnp.int32, codes.shape, 1) * side
+    column = jnp.sum(jnp.where(codes == code, place, 0).astype(F32))
+    return pl.multiple_of(column.astype(jnp.int32), side)
 
 
 def advance(half, level, ahead, flow_x, flow_y, celerity, above_x):
@@ -129,14 +112,11 @@
     return 1.0 + ids.astype(F32) * (2.0 / total_rows)
 
 
-def second_step(tile_count, plan_in, l_in, l_head, l_tail, halo, x_in, y_in, c, b, r,
-                x_out, y_out, l_out, held, drags, sums_out, plan, drag, plan_sem):
+def second_step(tile_count, l_in, l_head, l_tail, halo, x_in, y_in, c, b, r, x_out, y_out, l_out, d_out, sums_out):
     total, cols = l_in.shape
     half = cols // 2
     bands = total // BAND
     position = lax.axis_index("tile")
-    plan_copy = pltpu.make_async_copy(plan_in, plan, plan_sem)
-    plan_copy.start()
 
     def level_band(i):
         start, stop = i * BAND, (i + 1) * BAND
@@ -159,18 +139,16 @@
         x_out[rows] = new_x
         y_out[rows] = new_y
         l_out[rows] = new_level
-        drag[rows] = drag_of(r[rows], new_level, b[rows])
+        d_out[rows] = drag_of(r[rows], new_level, b[rows])
         for j in range(BAND // EDGE):
             if i + j > 0:
                 part = new_level[j * EDGE:(j + 1) * EDGE]
                 weight = row_weight(part.shape, position * total + i * BAND + j * EDGE, tile_count * total)
                 sums = sums + weight * (part * part)
     sums_out[...] = sums
-    plan_copy.wait()
-    put_blocks(plan, x_out, y_out, drag, held, drags)
-
-
-def second_edge(tile_count, row_count, plan, down, halo, l_head, l2_head, sums, b_head, r_head, drags_in, head, drags, shares):
+
+
+def second_edge(tile_count, row_count, down, halo, l_head, l2_head, sums, b_head, r_head, head, d_head, shares):
     cols = l_head.shape[1]
     half = cols // 2
     position = lax.axis_index("tile")
@@ -180,10 +158,7 @@
     row_ids = lax.broadcasted_iota(jnp.int32, (PACK, cols), 0)
     level = l2_head[...] + jnp.where(row_ids == 0, above_x, 0.0)
     head[...] = level
-    drag, codes = drag_of(r_head[...], level, b_head[...]).astype(F32), plan[...]
-    for slot in range(drags.shape[0]):
-        drags[slot] = drags_in[slot + 1]
-        drags[slot, 0:PACK] = of_code(slot + 1, codes, drag, drags.shape[-1]).astype(BF16)
+    d_head[...] = drag_of(r_head[...], level, b_head[...])
     top = level[:EDGE]
     whole = sums[...] + row_weight(top.shape, position * row_count, total_rows) * (top * top)
     lanes = lax.broadcasted_iota(jnp.int32, (1, 128), 1)
@@ -198,8 +173,8 @@
     for repeat in range(repeats):
         for slot in range(drags.shape[0]):
             for f in range(2):
-                start = source if repeat == 0 else held
-                mixed = jnp.dot(start[slot, f], smooth_t, preferred_element_type=F32).astype(BF16)
+                block = source(slot, f) if repeat == 0 else held[slot, f]
+                mixed = jnp.dot(block, smooth_t, preferred_element_type=F32).astype(BF16)
                 full = jnp.dot(smooth, mixed, preferred_element_type=F32)
                 settled = full / (1.0 + drags[slot].astype(F32) * jnp.abs(full))
                 if put is None or repeat + 1 < repeats:
@@ -208,10 +183,8 @@
                     put(slot, f, settled)
 
 
-def smooth_all(tile_count, plan_in, up, down, first, c, b, r, sm, sm_t, x_in, y_in, l_in, d_in,
-               x, y, l_head, l_tail, halo, x_last, held, drags, edge, low_x, plan, plan_sem):
-    plan_copy = pltpu.make_async_copy(plan_in, plan, plan_sem)
-    plan_copy.start()
+def smooth_all(tile_count, plan, up, down, first, c, b, r, sm, sm_t, x_in, y_in, l_in, d_in,
+               x, y, l_head, l_tail, halo, x_last, held, drags, edge, low_x):
     rows, cols = x.shape
     half = cols // 2
     side = sm.shape[0]
@@ -247,12 +220,12 @@
     first_edge, last_edge = pl.ds(0, PACK), pl.ds(PACK, PACK)
     edge[first_edge] = drag_of(r[first_rows], jnp.concatenate([top, l_in[pl.ds(EDGE, EDGE)]], 0), b[first_rows])
     edge[last_edge] = drag_of(r[last_rows], jnp.concatenate([l_in[pl.ds(rows - PACK, EDGE)], low], 0), b[last_rows])
-    plan_copy.wait()
-    dry = pl.ds(code_column(plan, 0, side), side)
+    codes = plan[...]
+    dry = pl.ds(code_column(codes, 0, side), side)
     x[:, dry] = x_in[:, dry]
     x[last_rows, dry] = low_x[:, dry]
     y[:, dry] = y_in[:, dry]
-    columns = [code_column(plan, code, side) for code in (1, 2, 3)]
+    columns = [code_column(codes, code, side) for code in (1, 2, 3)]
     for slot, column in enumerate(columns):
         span = pl.ds(column, side)
         drags[slot] = d_in[:, span]
@@ -265,54 +238,44 @@
     def put(slot, f, settled):
         (x, y)[f][:, pl.ds(columns[slot], side)] = settled
 
-    soften(sm[...], sm_t[...], held, held, drags, SUB, put)
+    soften(sm[...], sm_t[...], lambda slot, f: held[slot, f], held, drags, SUB, put)
     x_last[...] = x[rows - 1:rows]
 
 
-def start_last(repeats, sm, sm_t, held_in, drags, l_in, head, held, lev, sems):
-    rest, top = pl.ds(PACK, l_in.shape[0] - PACK), pl.ds(0, PACK)
-    copies = [
-        pltpu.make_async_copy(l_in.at[rest], lev.at[rest], sems.at[0]),
-        pltpu.make_async_copy(head.at[top], lev.at[top], sems.at[1]),
-    ]
-    for copy in copies:
-        copy.start()
-    soften(sm[...], sm_t[...], held_in.at[pl.ds(1, 3)], held, drags, repeats)
-    for copy in copies:
-        copy.wait()
-
-
-def go_on(repeats, sm, sm_t, held_in, drags, held):
-    soften(sm[...], sm_t[...], held_in, held, drags, repeats)
-
-
-def finish_last(repeats, plan_in, sm, sm_t, held_in, drags, x_in, y_in, x, y, own, near, far, held, plan, plan_sem):
-    plan_copy = pltpu.make_async_copy(plan_in, plan, plan_sem)
-    plan_copy.start()
+def start_last(repeats, plan, sm, sm_t, x, y, d, d_head, held, drags, edge):
     side = sm.shape[0]
-    columns = []
+    codes = plan[...]
+    edge[...] = d_head[...]
+    spans = [pl.ds(code_column(codes, code, side), side) for code in (1, 2, 3)]
+    for slot, span in enumerate(spans):
+        drags[slot] = d[:, span]
+        drags[slot, 0:PACK] = edge[:, span]
+    soften(sm[...], sm_t[...], lambda slot, f: (x, y)[f][:, spans[slot]].astype(BF16), held, drags, repeats)
+
+
+def finish_last(repeats, plan, sm, sm_t, held_in, drags, x_in, y_in, x, y, own, near, far, held):
+    side = sm.shape[0]
+    codes = plan[...]
+    dry, *spans = [pl.ds(code_column(codes, code, side), side) for code in range(4)]
 
     def put(slot, f, settled):
-        if not columns:
-            plan_copy.wait()
-            columns.extend(code_column(plan, code, side) for code in range(4))
-        (x, y)[f][:, pl.ds(columns[slot + 1], side)] = settled
+        (x, y)[f][:, spans[slot]] = settled
         if slot == 0:
             own[f] = settled
         else:
             (near, far)[slot - 1][f] = settled.astype(BF16)
 
-    soften(sm[...], sm_t[...], held_in, held, drags, repeats, put)
-    dry = pl.ds(columns[0], side)
+    soften(sm[...], sm_t[...], lambda slot, f: held_in[slot, f], held, drags, repeats, put)
     x[:, dry] = x_in[:, dry]
     y[:, dry] = y_in[:, dry]
 
 
-def put_fluxes(x_in, y_in, own, x, y, resident, sems):
-    copies = [
-        pltpu.make_async_copy(source, target, sems.at[i])
-        for i, (source, target) in enumerate(((x_in, x), (y_in, y), (own, resident.at[0])))
-    ]
+def put_fluxes(x_in, y_in, l_in, head, own, x, y, lev, resident, sems):
+    rest, top = pl.ds(PACK, l_in.shape[0] - PACK), pl.ds(0, PACK)
+    pairs = (
+        (x_in, x), (y_in, y), (own, resident.at[0]),
+        (l_in.at[rest], lev.at[rest]), (head.at[top], lev.at[top]))
+    copies = [pltpu.make_async_copy(source, target, sems.at[i]) for i, (source, target) in enumerate(pairs)]
     for copy in copies:
         copy.start()
     for copy in copies:
@@ -402,13 +365,11 @@
         return lax.ppermute(value, "tile", pairs)
 
     c, b, r, sm = celerity, bed_depth, roughness, smoother
-    codes = plan
-    surface, flux_x, flux_y, celerity, plan = [
+    surface, flux_x, flux_y, celerity = [
         pltpu.with_memory_space_constraint(array, pltpu.HBM)
-        for array in (surface, flux_x, flux_y, celerity, plan)
+        for array in (surface, flux_x, flux_y, celerity)
     ]
-    plan_scratch = [pltpu.SMEM(plan.shape, plan.dtype), pltpu.SemaphoreType.DMA]
-    held_shape, drag_shape = arr(4, 2, side, side, dtype=BF16), arr(4, side, side, dtype=BF16)
+    drag_shape = arr(rows, cols, dtype=BF16)
     wet_held, wet_drags = arr(3, 2, side, side, dtype=BF16), arr(3, side, side, dtype=BF16)
     up, down, first = call(
         edge_rows, "edge_rows", [HBM] * 4, (arr(5, cols), arr(7, cols), arr(1, cols)), [VMEM] * 3,
@@ -418,28 +379,27 @@
     down = moved(down, 1)
     x, y, lev, d, sm_t = call(
         first_step, "first_step", [HBM] * 3 + [VMEM] * 4,
-        (field, field, field, arr(rows, cols, dtype=BF16), square), [VMEM] * 5,
+        (field, field, field, drag_shape, square), [VMEM] * 5,
         (surface, flux_x, flux_y, c, b, r, sm),
         [pltpu.VMEM((rows, cols), F32)] * 3 + [pltpu.SemaphoreType.DMA((rows // LOAD, 3))],
         flops=20 * rows * cols, moved_bytes=24 * rows * cols)
     held_scratch, drag_scratch = pltpu.VMEM(wet_held.shape, BF16), pltpu.VMEM(wet_drags.shape, BF16)
     x, y, l_head, l_tail, halo, x_last = call(
-        lambda *refs: smooth_all(tiles, *refs), "smooth_all", [HBM] + [VMEM] * 12,
+        lambda *refs: smooth_all(tiles, *refs), "smooth_all", [VMEM] * 13,
         (field, field, arr(EDGE, cols), arr(EDGE, cols), arr(3, cols), arr(1, cols)), [VMEM] * 6,
         (plan, up, down, first, c, b, r, sm, sm_t, x, y, lev, d),
-        [held_scratch, drag_scratch, pltpu.VMEM((2 * PACK, cols), BF16), pltpu.VMEM((PACK, cols), F32)] + plan_scratch,
+        [held_scratch, drag_scratch, pltpu.VMEM((2 * PACK, cols), BF16), pltpu.VMEM((PACK, cols), F32)],
         flops=dots(6, SUB), moved_bytes=8 * rows * cols)
     down = moved(x_last, 1)
-    x, y, lev, held, drags, sums = call(
-        lambda *refs: second_step(tiles, *refs), "second_step", [HBM] + [VMEM] * 9,
-        (field, field, field, held_shape, drag_shape, arr(EDGE, cols)), [VMEM] * 6,
-        (plan, lev, l_head, l_tail, halo, x, y, c, b, r),
-        plan_scratch[:1] + [pltpu.VMEM((rows, cols), BF16)] + plan_scratch[1:],
+    x, y, lev, d, sums = call(
+        lambda *refs: second_step(tiles, *refs), "second_step", [VMEM] * 9,
+        (field, field, field, drag_shape, arr(EDGE, cols)), [VMEM] * 5,
+        (lev, l_head, l_tail, halo, x, y, c, b, r),
         flops=20 * rows * cols, moved_bytes=8 * rows * cols)
-    head, drags, shares = call(
-        lambda *refs: second_edge(tiles, rows, *refs), "second_edge", [VMEM] * 9,
-        (arr(PACK, cols), wet_drags, arr(1, 128)), [VMEM] * 3,
-        (codes, down, halo, l_head, lev[:PACK], sums, b[:PACK], r[:PACK], drags), flops=cols, moved_bytes=cols)
+    head, d_head, shares = call(
+        lambda *refs: second_edge(tiles, rows, *refs), "second_edge", [VMEM] * 7,
+        (arr(PACK, cols), arr(PACK, cols, dtype=BF16), arr(1, 128)), [VMEM] * 3,
+        (down, halo, l_head, lev[:PACK], sums, b[:PACK], r[:PACK]), flops=cols, moved_bytes=cols)
 
     stages = exchange_stages(tiles)
     done = 0
@@ -453,23 +413,20 @@
         return lax.optimization_barrier((shares + met,) + tuple(beside()))
 
     pair, resident_shape = arr(2, side, side, dtype=BF16), arr(3, 2, side, side)
-    shares, held, level = exchange(shares, lambda: call(
-        lambda *refs: start_last(PIECES[0], *refs), "start_last", [VMEM] * 6, (wet_held, field), [VMEM, HBM],
-        (sm, sm_t, held, drags, lev, head), [pltpu.SemaphoreType.DMA((2,))],
-        flops=dots(6, PIECES[0]), moved_bytes=rows * cols))
-    for piece in PIECES[1:-1]:
-        shares, held = exchange(shares, lambda: (call(
-            lambda *refs: go_on(piece, *refs), "go_on", [VMEM] * 4, wet_held, VMEM, (sm, sm_t, held, drags),
-            flops=dots(6, piece), moved_bytes=rows * cols),))
+    shares, held, drags = exchange(shares, lambda: call(
+        lambda *refs: start_last(HALF, *refs), "start_last", [VMEM] * 7, (wet_held, wet_drags), [VMEM] * 2,
+        (plan, sm, sm_t, x, y, d, d_head), [pltpu.VMEM((PACK, cols), BF16)],
+        flops=dots(6, HALF), moved_bytes=rows * cols))
     shares, x, y, own, near, far = exchange(shares, lambda: call(
-        lambda *refs: finish_last(PIECES[-1], *refs), "finish_last", [HBM] + [VMEM] * 6,
+        lambda *refs: finish_last(SUB - HALF, *refs), "finish_last", [VMEM] * 7,
         (field, field, arr(2, side, side), pair, pair), [VMEM] * 5,
-        (plan, sm, sm_t, held, drags, x, y), [held_scratch] + plan_scratch,
-        flops=dots(6, PIECES[-1]), moved_bytes=rows * cols))
-    near, far = moved(near, 1), moved(far, 2)
-    shares, x, y, resident = exchange(shares, lambda: call(
-        put_fluxes, "put_fluxes", [VMEM] * 3, (field, field, resident_shape), [HBM] * 3,
-        (x, y, own), [pltpu.SemaphoreType.DMA((3,))], moved_bytes=16 * rows * cols))
+        (plan, sm, sm_t, held, drags, x, y), [held_scratch],
+        flops=dots(6, SUB - HALF), moved_bytes=rows * cols))
+    far = moved(far, 2)
+    shares, x, y, level, resident, near = exchange(shares, lambda: tuple(call(
+        put_fluxes, "put_fluxes", [VMEM] * 5, (field, field, field, resident_shape), [HBM] * 4,
+        (x, y, lev, head, own), [pltpu.SemaphoreType.DMA((5,))], moved_bytes=16 * rows * cols)) + (near,))
+    near = moved(near, 1)
     while done + 1 < len(stages):
         shares, = exchange(shares, tuple)
     met = lax.ppermute(shares, "tile", stages[done])
@@ -477,6 +434,7 @@
         put_received, "put_received", [VMEM] * 2 + [HBM], resident_shape, HBM, (near, far, resident),
         [pltpu.VMEM((2, 2, side, side), F32), pltpu.SemaphoreType.DMA((2,))],
         aliases={2: 0}, moved_bytes=24 * side * side)
+    met, resident = lax.optimization_barrier((met, resident))
     energy = call(add_shares, "add_shares", [VMEM] * 2, arr(2), SMEM, (shares, met))
     return level, x, y, resident, energy
 

time: 52 us -> 49.3 us (0.948)
  the two profiles are of different devices: /device:TPU:1 before, /device:TPU:16 now
where the time goes in v3:
time: 49.3 us; the launch traced here: 49.2 us
  Pallas kernels  20.1 us (41%)
  waiting for transfers between devices  19.2 us (39%)
  starting transfers between devices  8.8 us (18%)
  between operations  1.01 us (2%)
    pallas_call x10, Pallas kernels, call(): pl.pallas_call(body, out_shape=outs, in_specs=ins, out_specs=out_specs, s...  20.1 us
    ppermute x5, waiting for transfers between devices, exchange(): met = lax.ppermute(shares, 'tile', stages[done])  11.7 us
    ppermute x5, starting transfers between devices, moved(): lax.ppermute(value, 'tile', [(i, (i + steps) % count) for i in range(coun...  7.74 us
    ppermute x5, waiting for transfers between devices, moved(): lax.ppermute(value, 'tile', [(i, (i + steps) % count) for i in range(coun...  7.5 us
  transfers between devices with their start and end apart: 11, of which 7 were waited for; matrix products, arithmetic and copies ran while one was open for 0% of the time, Pallas kernels for 26%

profile of v3, /device:TPU:16, one launch (start us, length us, event | category | flops | bytes accessed | tf_op | source)
XLA Modules:
  0.0 49.2 jit_solution(13569994480633455341)
XLA Ops:
  0.7 1.1 %edge_rows.1 = (f32[5,1024]{1,0:T(8,128)S(1)}, f32[7,1024]{1,0:T(8,128)S(1)}, f32[1,1024]{1,0:T(1,128)S(1)}) custom-call(f32[256,1024]{1,0:T(8,128)} %s_in.1, f32[256,1024]{1,0:T(8,128)} %x_in.1, f32[256,1024]{1,0:T(8,128)} %y_in.1, f32[256,1024]{1,0:T(8,128)} %refs_6_.3), custom_call_target="tpu_custom_call" | custom-call | tf_op jit(solution)/shard_map/edge_rows/pallas_call | solution.py:349
  1.8 0.1 collective-permute-start.1
  1.9 0.0 copy-start.4
  1.9 7.6 %collective-permute-start = (f32[5,1024]{1,0:T(8,128)S(1)}, f32[5,1024]{1,0:T(8,128)S(1)}, u32[]{:S(2)}, u32[]{:S(2)}) collective-permute-start(f32[5,1024]{1,0:T(8,128)S(1)} %get-tuple-element.55), channel_id=1, source_target_pairs={{0,63},{1,0},{2,1},{3,2},{4,3},{5,4},{6,5},{7,6},{8,7},{9,8},{10,9... | collective-permute-start | bytes 61448 | tf_op jit(solution)/shard_map/ppermute | solution.py:304
  9.5 2.6 %first_step.1 = (f32[256,1024]{1,0:T(8,128)S(1)}, f32[256,1024]{1,0:T(8,128)S(1)}, f32[256,1024]{1,0:T(8,128)S(1)}, bf16[256,1024]{1,0:T(8,128)(2,1)S(1)}, bf16[256,256]{1,0:T(8,128)(2,1)S(1)}) custom-call(f32[256,1024]{1,0:T(8,128)} %s_in.1, f32[256,1024]{1,0:T(8,128)} %x_in.1, f32[256,1024]{1,0:T(8,128)} %y_in.1, f32[256,1024]{1,0:T(8,128)S(1)} %copy-done, ...), custom_call_target="tpu_custom_call" | custom-call | flops 5242880 | bytes 6291456 | tf_op jit(solution)/shard_map/first_step/pallas_call | solution.py:349
  12.1 0.0 collective-permute-done.refs_1_
  12.1 0.0 collective-permute-done.1.refs_2_
  12.1 5.6 %smooth_all.1 = (f32[256,1024]{1,0:T(8,128)S(1)}, f32[256,1024]{1,0:T(8,128)S(1)}, f32[8,1024]{1,0:T(8,128)S(1)}, f32[8,1024]{1,0:T(8,128)S(1)}, f32[3,1024]{1,0:T(4,128)S(1)}, /*index=5*/f32[1,1024]{1,0:T(1,128)S(1)}) custom-call(s32[1,4]{1,0:T(1,128)S(1)} %copy-done.4, f32[5,1024]{1,0:T(8,128)S(1)} %collective-permute-done.refs_1_, ...), custom_call_target="tpu_custom_call" | custom-call | flops 4831838208 | bytes 2097152 | tf_op jit(solution)/shard_map/smooth_all/pallas_call | solution.py:349
  17.7 0.1 collective-permute-start.2
  17.8 1.2 %second_step.1 = (f32[256,1024]{1,0:T(8,128)S(1)}, f32[256,1024]{1,0:T(8,128)S(1)}, f32[256,1024]{1,0:T(8,128)S(1)}, bf16[256,1024]{1,0:T(8,128)(2,1)S(1)}, f32[8,1024]{1,0:T(8,128)S(1)}) custom-call(f32[256,1024]{1,0:T(8,128)S(1)} %get-tuple-element.61.refs_11_.refs_0_, f32[8,1024]{1,0:T(8,128)S(1)} %get-tuple-element.65.refs_1_.refs_2_, ...), custom_call_target="tpu_custom_call" | custom-call | flops 5242880 | bytes 2097152 | tf_op jit(solution)/shard_map/second_step/pallas_call | solution.py:349
  19.1 5.0 %collective-permute-done.2.refs_0_ = f32[1,1024]{1,0:T(1,128)S(1)} collective-permute-done((f32[1,1024]{1,0:T(1,128)S(1)}, f32[1,1024]{1,0:T(1,128)S(1)}, u32[]{:S(2)}, u32[]{:S(2)}) %collective-permute-start.2) | collective-permute-done | bytes 4128 | tf_op jit(solution)/shard_map/ppermute | solution.py:304
  24.2 0.1 second_edge.1
  24.3 0.3 collective-permute-start.3
  24.6 3.0 %start_last.1 = (bf16[3,2,256,256]{3,2,1,0:T(8,128)(2,1)S(1)}, bf16[3,256,256]{2,1,0:T(8,128)(2,1)S(1)}) custom-call(s32[1,4]{1,0:T(1,128)S(1)} %copy-done.4, bf16[256,256]{1,0:T(8,128)(2,1)S(1)} %copy-done.3, bf16[256,256]{1,0:T(8,128)(2,1)S(1)} %get-tuple-element.58.refs_8_.refs_2_, f32[256,1024]{1,0:T(8,128)S(1)} %get-tuple-element.72.refs_3_.refs_5_, ...), custom_call_target="tpu_custom_call" | custom-call | flops 2415919104 | bytes 262144 | tf_op jit(solution)/shard_map/start_last/pallas_call | solution.py:349
  27.6 1.5 %collective-permute-done.3 = f32[1,128]{1,0:T(1,128)S(1)} collective-permute-done((f32[1,128]{1,0:T(1,128)S(1)}, f32[1,128]{1,0:T(1,128)S(1)}, u32[]{:S(2)}, u32[]{:S(2)}) %collective-permute-start.3) | collective-permute-done | bytes 544 | tf_op jit(solution)/shard_map/ppermute | solution.py:411
  29.0 0.0 collective-permute-start.4
  29.0 2.9 %finish_last.1 = (f32[256,1024]{1,0:T(8,128)S(1)}, f32[256,1024]{1,0:T(8,128)S(1)}, f32[2,256,256]{2,1,0:T(8,128)S(1)}, bf16[2,256,256]{2,1,0:T(8,128)(2,1)S(1)}, bf16[2,256,256]{2,1,0:T(8,128)(2,1)S(1)}) custom-call(s32[1,4]{1,0:T(1,128)S(1)} %copy-done.4, bf16[256,256]{1,0:T(8,128)(2,1)S(1)} %copy-done.3, ...), custom_call_target="tpu_custom_call" | custom-call | flops 2415919104 | bytes 262144 | tf_op jit(solution)/shard_map/finish_last/pallas_call | solution.py:349
  32.0 2.7 %collective-permute-done.4 = f32[1,128]{1,0:T(1,128)S(1)} collective-permute-done((f32[1,128]{1,0:T(1,128)S(1)}, f32[1,128]{1,0:T(1,128)S(1)}, u32[]{:S(2)}, u32[]{:S(2)}) %collective-permute-start.4) | collective-permute-done | bytes 544 | tf_op jit(solution)/shard_map/ppermute | solution.py:411
  34.7 0.0 collective-permute-start.5
  34.7 0.0 collective-permute-start.10
  34.7 1.9 %put_fluxes.1 = (f32[256,1024]{1,0:T(8,128)}, f32[256,1024]{1,0:T(8,128)}, f32[256,1024]{1,0:T(8,128)}, f32[3,2,256,256]{3,2,1,0:T(8,128)}) custom-call(f32[256,1024]{1,0:T(8,128)S(1)} %get-tuple-element.87.x_in, f32[256,1024]{1,0:T(8,128)S(1)} %get-tuple-element.88.y_in, f32[256,1024]{1,0:T(8,128)S(1)} %get-tuple-element.69.l_in, ...), custom_call_target="tpu_custom_call" | custom-call | bytes 4194304 | tf_op jit(solution)/shard_map/put_fluxes/pallas_call | solution.py:349
  36.6 1.7 %collective-permute-done.5 = f32[1,128]{1,0:T(1,128)S(1)} collective-permute-done((f32[1,128]{1,0:T(1,128)S(1)}, f32[1,128]{1,0:T(1,128)S(1)}, u32[]{:S(2)}, u32[]{:S(2)}) %collective-permute-start.5) | collective-permute-done | bytes 544 | tf_op jit(solution)/shard_map/ppermute | solution.py:411
  38.2 0.0 collective-permute-start.9
  38.2 0.0 collective-permute-start.6
  38.2 4.7 %collective-permute-done.6 = f32[1,128]{1,0:T(1,128)S(1)} collective-permute-done((f32[1,128]{1,0:T(1,128)S(1)}, f32[1,128]{1,0:T(1,128)S(1)}, u32[]{:S(2)}, u32[]{:S(2)}) %collective-permute-start.6) | collective-permute-done | bytes 544 | tf_op jit(solution)/shard_map/ppermute | solution.py:411
  43.0 0.0 collective-permute-start.7
  43.0 1.1 %collective-permute-done.7 = f32[1,128]{1,0:T(1,128)S(1)} collective-permute-done((f32[1,128]{1,0:T(1,128)S(1)}, f32[1,128]{1,0:T(1,128)S(1)}, u32[]{:S(2)}, u32[]{:S(2)}) %collective-permute-start.7) | collective-permute-done | bytes 544 | tf_op jit(solution)/shard_map/ppermute | solution.py:411
  44.1 0.8 %collective-permute-start.8 = (f32[1,128]{1,0:T(1,128)S(1)}, f32[1,128]{1,0:T(1,128)S(1)}, u32[]{:S(2)}, u32[]{:S(2)}) collective-permute-start(f32[1,128]{1,0:T(1,128)S(1)} %add.19.mine), channel_id=1, source_target_pairs={{0,2},{1,3},{2,0},{3,1},{4,6},{5,7},{6,4},{7,5},{8,10},{9,11},{10,... | collective-permute-start | bytes 1544 | tf_op jit(solution)/shard_map/ppermute | solution.py:432
  44.9 0.0 collective-permute-done.10.far
  44.9 2.4 %collective-permute-done.9.near = bf16[2,256,256]{2,1,0:T(8,128)(2,1)S(1)} collective-permute-done((bf16[2,256,256]{2,1,0:T(8,128)(2,1)S(1)}, bf16[2,256,256]{2,1,0:T(8,128)(2,1)S(1)}, u32[]{:S(2)}, u32[]{:S(2)}) %collective-permute-start.9) | collective-permute-done | bytes 262176 | tf_op jit(solution)/shard_map/ppermute | solution.py:304
  47.3 1.0 %put_received.1 = f32[3,2,256,256]{3,2,1,0:T(8,128)} custom-call(bf16[2,256,256]{2,1,0:T(8,128)(2,1)S(1)} %collective-permute-done.9.near, bf16[2,256,256]{2,1,0:T(8,128)(2,1)S(1)} %collective-permute-done.10.far, f32[3,2,256,256]{3,2,1,0:T(8,128)} %get-tuple-element.102.resident_held), custom_call_target="tpu_custom_call", output_to_operand_aliasing={{}: (2, {})} | custom-call | bytes 1572864 | tf_op jit(solution)/shard_map/put_received/pallas_call | solution.py:349
  48.4 0.6 %add_shares.1 = f32[2]{0:T(128)} custom-call(f32[1,128]{1,0:T(1,128)S(1)} %add.19.mine, f32[1,128]{1,0:T(1,128)S(1)} %collective-permute-done.8.received), custom_call_target="tpu_custom_call" | custom-call | tf_op jit(solution)/shard_map/add_shares/pallas_call | solution.py:349
  (18 shorter events, 0.1 us)
Async XLA Ops:
  0.6 8.8 %copy-start = (f32[256,1024]{1,0:T(8,128)S(1)}, f32[256,1024]{1,0:T(8,128)}, u32[]{:S(2)}) copy-start(f32[256,1024]{1,0:T(8,128)} %refs_6_.3) | copy-start | bytes 3145732
  0.6 8.8 %copy-start.3 = (bf16[256,256]{1,0:T(8,128)(2,1)S(1)}, bf16[256,256]{1,0:T(8,128)(2,1)}, u32[]{:S(2)}) copy-start(bf16[256,256]{1,0:T(8,128)(2,1)} %refs_1_.3) | copy-start | bytes 393220
  0.7 8.8 %copy-start.2 = (f32[256,1024]{1,0:T(8,128)S(1)}, f32[256,1024]{1,0:T(8,128)}, u32[]{:S(2)}) copy-start(f32[256,1024]{1,0:T(8,128)} %refs_8_.1) | copy-start | bytes 3145732
  0.7 8.8 %copy-start.1 = (f32[256,1024]{1,0:T(8,128)S(1)}, f32[256,1024]{1,0:T(8,128)}, u32[]{:S(2)}) copy-start(f32[256,1024]{1,0:T(8,128)} %refs_7_.3) | copy-start | bytes 3145732
  1.8 10.3 %collective-permute-start.1 = (f32[7,1024]{1,0:T(8,128)S(1)}, f32[7,1024]{1,0:T(8,128)S(1)}, u32[]{:S(2)}, u32[]{:S(2)}) collective-permute-start(f32[7,1024]{1,0:T(8,128)S(1)} %get-tuple-element.56), channel_id=1, source_target_pairs={{0,1},{1,2},{2,3},{3,4},{4,5},{5,6},{6,7},{7,8},{8,9},{9,10},{10,1... | collective-permute-start | bytes 86024 | tf_op jit(solution)/shard_map/ppermute | solution.py:304
  1.9 10.2 %copy-start.4 = (s32[1,4]{1,0:T(1,128)S(1)}, s32[1,4]{1,0:T(1,128)}, u32[]{:S(2)}) copy-start(s32[1,4]{1,0:T(1,128)} %refs_0_.5) | copy-start | bytes 52
  1.9 10.2 %collective-permute-start = (f32[5,1024]{1,0:T(8,128)S(1)}, f32[5,1024]{1,0:T(8,128)S(1)}, u32[]{:S(2)}, u32[]{:S(2)}) collective-permute-start(f32[5,1024]{1,0:T(8,128)S(1)} %get-tuple-element.55), channel_id=1, source_target_pairs={{0,63},{1,0},{2,1},{3,2},{4,3},{5,4},{6,5},{7,6},{8,7},{9,8},{10,9... | collective-permute-start | bytes 61448 | tf_op jit(solution)/shard_map/ppermute | solution.py:304
  17.7 6.4 %collective-permute-start.2 = (f32[1,1024]{1,0:T(1,128)S(1)}, f32[1,1024]{1,0:T(1,128)S(1)}, u32[]{:S(2)}, u32[]{:S(2)}) collective-permute-start(f32[1,1024]{1,0:T(1,128)S(1)} %get-tuple-element.63), channel_id=1, source_target_pairs={{0,1},{1,2},{2,3},{3,4},{4,5},{5,6},{6,7},{7,8},{8,9},{9,10},{10,1... | collective-permute-start | bytes 12296 | tf_op jit(solution)/shard_map/ppermute | solution.py:304
  24.3 4.7 %collective-permute-start.3 = (f32[1,128]{1,0:T(1,128)S(1)}, f32[1,128]{1,0:T(1,128)S(1)}, u32[]{:S(2)}, u32[]{:S(2)}) collective-permute-start(f32[1,128]{1,0:T(1,128)S(1)} %get-tuple-element.71), channel_id=1, source_target_pairs={{0,4},{1,5},{2,6},{3,7},{4,0},{5,1},{6,2},{7,3},{8,12},{9,13},{10,... | collective-permute-start | bytes 1544 | tf_op jit(solution)/shard_map/ppermute | solution.py:411
  29.0 5.7 %collective-permute-start.4 = (f32[1,128]{1,0:T(1,128)S(1)}, f32[1,128]{1,0:T(1,128)S(1)}, u32[]{:S(2)}, u32[]{:S(2)}) collective-permute-start(f32[1,128]{1,0:T(1,128)S(1)} %add.15), channel_id=1, source_target_pairs={{0,12},{1,13},{2,14},{3,15},{4,8},{5,9},{6,10},{7,11},{8,4},{9,5},... | collective-permute-start | bytes 1544 | tf_op jit(solution)/shard_map/ppermute | solution.py:411
  34.7 3.5 %collective-permute-start.5 = (f32[1,128]{1,0:T(1,128)S(1)}, f32[1,128]{1,0:T(1,128)S(1)}, u32[]{:S(2)}, u32[]{:S(2)}) collective-permute-start(f32[1,128]{1,0:T(1,128)S(1)} %add.16), channel_id=1, source_target_pairs={{0,16},{1,17},{2,18},{3,19},{4,20},{5,21},{6,22},{7,23},{8,24},{9,... | collective-permute-start | bytes 1544 | tf_op jit(solution)/shard_map/ppermute | solution.py:411
  34.7 10.2 %collective-permute-start.10 = (bf16[2,256,256]{2,1,0:T(8,128)(2,1)S(1)}, bf16[2,256,256]{2,1,0:T(8,128)(2,1)S(1)}, u32[]{:S(2)}, u32[]{:S(2)}) collective-permute-start(bf16[2,256,256]{2,1,0:T(8,128)(2,1)S(1)} %get-tuple-element.101), channel_id=1, source_target_pairs={{0,2},{1,3},{2,4},{3,5},{4,6},{5,7},{6,8},{7,9},{8,10},{9,11},{10,... | collective-permute-start | bytes 786440 | tf_op jit(solution)/shard_map/ppermute | solution.py:304
  38.2 9.1 %collective-permute-start.9 = (bf16[2,256,256]{2,1,0:T(8,128)(2,1)S(1)}, bf16[2,256,256]{2,1,0:T(8,128)(2,1)S(1)}, u32[]{:S(2)}, u32[]{:S(2)}) collective-permute-start(bf16[2,256,256]{2,1,0:T(8,128)(2,1)S(1)} %get-tuple-element.100), channel_id=1, source_target_pairs={{0,1},{1,2},{2,3},{3,4},{4,5},{5,6},{6,7},{7,8},{8,9},{9,10},{10,1... | collective-permute-start | bytes 786440 | tf_op jit(solution)/shard_map/ppermute | solution.py:304
  38.2 4.8 %collective-permute-start.6 = (f32[1,128]{1,0:T(1,128)S(1)}, f32[1,128]{1,0:T(1,128)S(1)}, u32[]{:S(2)}, u32[]{:S(2)}) collective-permute-start(f32[1,128]{1,0:T(1,128)S(1)} %add.17), channel_id=1, source_target_pairs={{0,48},{1,49},{2,50},{3,51},{4,52},{5,53},{6,54},{7,55},{8,56},{9,... | collective-permute-start | bytes 1544 | tf_op jit(solution)/shard_map/ppermute | solution.py:411
  43.0 1.1 %collective-permute-start.7 = (f32[1,128]{1,0:T(1,128)S(1)}, f32[1,128]{1,0:T(1,128)S(1)}, u32[]{:S(2)}, u32[]{:S(2)}) collective-permute-start(f32[1,128]{1,0:T(1,128)S(1)} %add.18), channel_id=1, source_target_pairs={{0,1},{1,0},{2,3},{3,2},{4,5},{5,4},{6,7},{7,6},{8,9},{9,8},{10,11... | collective-permute-start | bytes 1544 | tf_op jit(solution)/shard_map/ppermute | solution.py:411
  44.1 4.3 %collective-permute-start.8 = (f32[1,128]{1,0:T(1,128)S(1)}, f32[1,128]{1,0:T(1,128)S(1)}, u32[]{:S(2)}, u32[]{:S(2)}) collective-permute-start(f32[1,128]{1,0:T(1,128)S(1)} %add.19.mine), channel_id=1, source_target_pairs={{0,2},{1,3},{2,0},{3,1},{4,6},{5,7},{6,4},{7,5},{8,10},{9,11},{10,... | collective-permute-start | bytes 1544 | tf_op jit(solution)/shard_map/ppermute | solution.py:432

commit v4 on v3

--- a/solution.py
+++ b/solution.py
@@ -6,7 +6,7 @@
 from jax.sharding import PartitionSpec as P
 
 SUB = 12
-HALF = 6
+HALF = 5
 EDGE = 8
 PACK = 16
 BAND = 32

time: 49.3 us -> 49.3 us (level)
  no operation moved by 1% of the time
where the time goes in v4:
time: 49.3 us; the launch traced here: 49.2 us
  Pallas kernels  20.2 us (41%)
  waiting for transfers between devices  19.6 us (40%)
  starting transfers between devices  8.38 us (17%)
  between operations  1 us (2%)
    pallas_call x10, Pallas kernels, call(): pl.pallas_call(body, out_shape=outs, in_specs=ins, out_specs=out_specs, s...  20.2 us
    ppermute x5, waiting for transfers between devices, exchange(): met = lax.ppermute(shares, 'tile', stages[done])  11.7 us
    ppermute x5, waiting for transfers between devices, moved(): lax.ppermute(value, 'tile', [(i, (i + steps) % count) for i in range(coun...  7.92 us
    ppermute x5, starting transfers between devices, moved(): lax.ppermute(value, 'tile', [(i, (i + steps) % count) for i in range(coun...  7.74 us
  transfers between devices with their start and end apart: 11, of which 7 were waited for; matrix products, arithmetic and copies ran while one was open for 0% of the time, Pallas kernels for 26%

profile of v4, /device:TPU:16, one launch (start us, length us, event | category | flops | bytes accessed | tf_op | source)
XLA Modules:
  0.0 49.2 jit_solution(2231949099272876478)
XLA Ops:
  0.7 1.1 %edge_rows.1 = (f32[5,1024]{1,0:T(8,128)S(1)}, f32[7,1024]{1,0:T(8,128)S(1)}, f32[1,1024]{1,0:T(1,128)S(1)}) custom-call(f32[256,1024]{1,0:T(8,128)} %s_in.1, f32[256,1024]{1,0:T(8,128)} %x_in.1, f32[256,1024]{1,0:T(8,128)} %y_in.1, f32[256,1024]{1,0:T(8,128)} %refs_6_.3), custom_call_target="tpu_custom_call" | custom-call | tf_op jit(solution)/shard_map/edge_rows/pallas_call | solution.py:349
  1.8 0.1 collective-permute-start.1
  1.9 0.0 copy-start.4
  1.9 7.6 %collective-permute-start = (f32[5,1024]{1,0:T(8,128)S(1)}, f32[5,1024]{1,0:T(8,128)S(1)}, u32[]{:S(2)}, u32[]{:S(2)}) collective-permute-start(f32[5,1024]{1,0:T(8,128)S(1)} %get-tuple-element.55), channel_id=1, source_target_pairs={{0,63},{1,0},{2,1},{3,2},{4,3},{5,4},{6,5},{7,6},{8,7},{9,8},{10,9... | collective-permute-start | bytes 61448 | tf_op jit(solution)/shard_map/ppermute | solution.py:304
  9.5 2.6 %first_step.1 = (f32[256,1024]{1,0:T(8,128)S(1)}, f32[256,1024]{1,0:T(8,128)S(1)}, f32[256,1024]{1,0:T(8,128)S(1)}, bf16[256,1024]{1,0:T(8,128)(2,1)S(1)}, bf16[256,256]{1,0:T(8,128)(2,1)S(1)}) custom-call(f32[256,1024]{1,0:T(8,128)} %s_in.1, f32[256,1024]{1,0:T(8,128)} %x_in.1, f32[256,1024]{1,0:T(8,128)} %y_in.1, f32[256,1024]{1,0:T(8,128)S(1)} %copy-done, ...), custom_call_target="tpu_custom_call" | custom-call | flops 5242880 | bytes 6291456 | tf_op jit(solution)/shard_map/first_step/pallas_call | solution.py:349
  12.1 0.0 collective-permute-done.refs_1_
  12.1 0.0 collective-permute-done.1.refs_2_
  12.1 5.6 %smooth_all.1 = (f32[256,1024]{1,0:T(8,128)S(1)}, f32[256,1024]{1,0:T(8,128)S(1)}, f32[8,1024]{1,0:T(8,128)S(1)}, f32[8,1024]{1,0:T(8,128)S(1)}, f32[3,1024]{1,0:T(4,128)S(1)}, /*index=5*/f32[1,1024]{1,0:T(1,128)S(1)}) custom-call(s32[1,4]{1,0:T(1,128)S(1)} %copy-done.4, f32[5,1024]{1,0:T(8,128)S(1)} %collective-permute-done.refs_1_, ...), custom_call_target="tpu_custom_call" | custom-call | flops 4831838208 | bytes 2097152 | tf_op jit(solution)/shard_map/smooth_all/pallas_call | solution.py:349
  17.7 0.1 collective-permute-start.2
  17.9 1.2 %second_step.1 = (f32[256,1024]{1,0:T(8,128)S(1)}, f32[256,1024]{1,0:T(8,128)S(1)}, f32[256,1024]{1,0:T(8,128)S(1)}, bf16[256,1024]{1,0:T(8,128)(2,1)S(1)}, f32[8,1024]{1,0:T(8,128)S(1)}) custom-call(f32[256,1024]{1,0:T(8,128)S(1)} %get-tuple-element.61.refs_11_.refs_0_, f32[8,1024]{1,0:T(8,128)S(1)} %get-tuple-element.65.refs_1_.refs_2_, ...), custom_call_target="tpu_custom_call" | custom-call | flops 5242880 | bytes 2097152 | tf_op jit(solution)/shard_map/second_step/pallas_call | solution.py:349
  19.1 5.0 %collective-permute-done.2.refs_0_ = f32[1,1024]{1,0:T(1,128)S(1)} collective-permute-done((f32[1,1024]{1,0:T(1,128)S(1)}, f32[1,1024]{1,0:T(1,128)S(1)}, u32[]{:S(2)}, u32[]{:S(2)}) %collective-permute-start.2) | collective-permute-done | bytes 4128 | tf_op jit(solution)/shard_map/ppermute | solution.py:304
  24.2 0.1 second_edge.1
  24.3 0.3 collective-permute-start.3
  24.6 2.6 %start_last.1 = (bf16[3,2,256,256]{3,2,1,0:T(8,128)(2,1)S(1)}, bf16[3,256,256]{2,1,0:T(8,128)(2,1)S(1)}) custom-call(s32[1,4]{1,0:T(1,128)S(1)} %copy-done.4, bf16[256,256]{1,0:T(8,128)(2,1)S(1)} %copy-done.3, bf16[256,256]{1,0:T(8,128)(2,1)S(1)} %get-tuple-element.58.refs_8_.refs_2_, f32[256,1024]{1,0:T(8,128)S(1)} %get-tuple-element.72.refs_3_.refs_5_, ...), custom_call_target="tpu_custom_call" | custom-call | flops 2013265920 | bytes 262144 | tf_op jit(solution)/shard_map/start_last/pallas_call | solution.py:349
  27.2 1.9 %collective-permute-done.3 = f32[1,128]{1,0:T(1,128)S(1)} collective-permute-done((f32[1,128]{1,0:T(1,128)S(1)}, f32[1,128]{1,0:T(1,128)S(1)}, u32[]{:S(2)}, u32[]{:S(2)}) %collective-permute-start.3) | collective-permute-done | bytes 544 | tf_op jit(solution)/shard_map/ppermute | solution.py:411
  29.0 0.0 collective-permute-start.4
  29.0 3.4 %finish_last.1 = (f32[256,1024]{1,0:T(8,128)S(1)}, f32[256,1024]{1,0:T(8,128)S(1)}, f32[2,256,256]{2,1,0:T(8,128)S(1)}, bf16[2,256,256]{2,1,0:T(8,128)(2,1)S(1)}, bf16[2,256,256]{2,1,0:T(8,128)(2,1)S(1)}) custom-call(s32[1,4]{1,0:T(1,128)S(1)} %copy-done.4, bf16[256,256]{1,0:T(8,128)(2,1)S(1)} %copy-done.3, ...), custom_call_target="tpu_custom_call" | custom-call | flops 2818572288 | bytes 262144 | tf_op jit(solution)/shard_map/finish_last/pallas_call | solution.py:349
  32.4 2.3 %collective-permute-done.4 = f32[1,128]{1,0:T(1,128)S(1)} collective-permute-done((f32[1,128]{1,0:T(1,128)S(1)}, f32[1,128]{1,0:T(1,128)S(1)}, u32[]{:S(2)}, u32[]{:S(2)}) %collective-permute-start.4) | collective-permute-done | bytes 544 | tf_op jit(solution)/shard_map/ppermute | solution.py:411
  34.7 0.0 collective-permute-start.5
  34.7 0.0 collective-permute-start.10
  34.7 1.9 %put_fluxes.1 = (f32[256,1024]{1,0:T(8,128)}, f32[256,1024]{1,0:T(8,128)}, f32[256,1024]{1,0:T(8,128)}, f32[3,2,256,256]{3,2,1,0:T(8,128)}) custom-call(f32[256,1024]{1,0:T(8,128)S(1)} %get-tuple-element.87.x_in, f32[256,1024]{1,0:T(8,128)S(1)} %get-tuple-element.88.y_in, f32[256,1024]{1,0:T(8,128)S(1)} %get-tuple-element.69.l_in, ...), custom_call_target="tpu_custom_call" | custom-call | bytes 4194304 | tf_op jit(solution)/shard_map/put_fluxes/pallas_call | solution.py:349
  36.6 1.7 %collective-permute-done.5 = f32[1,128]{1,0:T(1,128)S(1)} collective-permute-done((f32[1,128]{1,0:T(1,128)S(1)}, f32[1,128]{1,0:T(1,128)S(1)}, u32[]{:S(2)}, u32[]{:S(2)}) %collective-permute-start.5) | collective-permute-done | bytes 544 | tf_op jit(solution)/shard_map/ppermute | solution.py:411
  38.2 0.0 collective-permute-start.9
  38.2 4.7 %collective-permute-done.6 = f32[1,128]{1,0:T(1,128)S(1)} collective-permute-done((f32[1,128]{1,0:T(1,128)S(1)}, f32[1,128]{1,0:T(1,128)S(1)}, u32[]{:S(2)}, u32[]{:S(2)}) %collective-permute-start.6) | collective-permute-done | bytes 544 | tf_op jit(solution)/shard_map/ppermute | solution.py:411
  43.0 0.0 collective-permute-start.7
  43.0 1.1 %collective-permute-done.7 = f32[1,128]{1,0:T(1,128)S(1)} collective-permute-done((f32[1,128]{1,0:T(1,128)S(1)}, f32[1,128]{1,0:T(1,128)S(1)}, u32[]{:S(2)}, u32[]{:S(2)}) %collective-permute-start.7) | collective-permute-done | bytes 544 | tf_op jit(solution)/shard_map/ppermute | solution.py:411
  44.1 0.4 collective-permute-start.8
  44.5 0.0 collective-permute-done.10.far
  44.5 2.9 %collective-permute-done.9.near = bf16[2,256,256]{2,1,0:T(8,128)(2,1)S(1)} collective-permute-done((bf16[2,256,256]{2,1,0:T(8,128)(2,1)S(1)}, bf16[2,256,256]{2,1,0:T(8,128)(2,1)S(1)}, u32[]{:S(2)}, u32[]{:S(2)}) %collective-permute-start.9) | collective-permute-done | bytes 262176 | tf_op jit(solution)/shard_map/ppermute | solution.py:304
  47.4 1.0 %put_received.1 = f32[3,2,256,256]{3,2,1,0:T(8,128)} custom-call(bf16[2,256,256]{2,1,0:T(8,128)(2,1)S(1)} %collective-permute-done.9.near, bf16[2,256,256]{2,1,0:T(8,128)(2,1)S(1)} %collective-permute-done.10.far, f32[3,2,256,256]{3,2,1,0:T(8,128)} %get-tuple-element.102.resident_held), custom_call_target="tpu_custom_call", output_to_operand_aliasing={{}: (2, {})} | custom-call | bytes 1572864 | tf_op jit(solution)/shard_map/put_received/pallas_call | solution.py:349
  48.4 0.0 collective-permute-done.8.received
  48.4 0.6 %add_shares.1 = f32[2]{0:T(128)} custom-call(f32[1,128]{1,0:T(1,128)S(1)} %add.19.mine, f32[1,128]{1,0:T(1,128)S(1)} %collective-permute-done.8.received), custom_call_target="tpu_custom_call" | custom-call | tf_op jit(solution)/shard_map/add_shares/pallas_call | solution.py:349
  (18 shorter events, 0.1 us)
Async XLA Ops:
  0.6 8.8 %copy-start = (f32[256,1024]{1,0:T(8,128)S(1)}, f32[256,1024]{1,0:T(8,128)}, u32[]{:S(2)}) copy-start(f32[256,1024]{1,0:T(8,128)} %refs_6_.3) | copy-start | bytes 3145732
  0.6 8.8 %copy-start.3 = (bf16[256,256]{1,0:T(8,128)(2,1)S(1)}, bf16[256,256]{1,0:T(8,128)(2,1)}, u32[]{:S(2)}) copy-start(bf16[256,256]{1,0:T(8,128)(2,1)} %refs_1_.3) | copy-start | bytes 393220
  0.7 8.8 %copy-start.2 = (f32[256,1024]{1,0:T(8,128)S(1)}, f32[256,1024]{1,0:T(8,128)}, u32[]{:S(2)}) copy-start(f32[256,1024]{1,0:T(8,128)} %refs_8_.1) | copy-start | bytes 3145732
  0.7 8.8 %copy-start.1 = (f32[256,1024]{1,0:T(8,128)S(1)}, f32[256,1024]{1,0:T(8,128)}, u32[]{:S(2)}) copy-start(f32[256,1024]{1,0:T(8,128)} %refs_7_.3) | copy-start | bytes 3145732
  1.8 10.3 %collective-permute-start.1 = (f32[7,1024]{1,0:T(8,128)S(1)}, f32[7,1024]{1,0:T(8,128)S(1)}, u32[]{:S(2)}, u32[]{:S(2)}) collective-permute-start(f32[7,1024]{1,0:T(8,128)S(1)} %get-tuple-element.56), channel_id=1, source_target_pairs={{0,1},{1,2},{2,3},{3,4},{4,5},{5,6},{6,7},{7,8},{8,9},{9,10},{10,1... | collective-permute-start | bytes 86024 | tf_op jit(solution)/shard_map/ppermute | solution.py:304
  1.9 10.2 %copy-start.4 = (s32[1,4]{1,0:T(1,128)S(1)}, s32[1,4]{1,0:T(1,128)}, u32[]{:S(2)}) copy-start(s32[1,4]{1,0:T(1,128)} %refs_0_.5) | copy-start | bytes 52
  1.9 10.2 %collective-permute-start = (f32[5,1024]{1,0:T(8,128)S(1)}, f32[5,1024]{1,0:T(8,128)S(1)}, u32[]{:S(2)}, u32[]{:S(2)}) collective-permute-start(f32[5,1024]{1,0:T(8,128)S(1)} %get-tuple-element.55), channel_id=1, source_target_pairs={{0,63},{1,0},{2,1},{3,2},{4,3},{5,4},{6,5},{7,6},{8,7},{9,8},{10,9... | collective-permute-start | bytes 61448 | tf_op jit(solution)/shard_map/ppermute | solution.py:304
  17.7 6.4 %collective-permute-start.2 = (f32[1,1024]{1,0:T(1,128)S(1)}, f32[1,1024]{1,0:T(1,128)S(1)}, u32[]{:S(2)}, u32[]{:S(2)}) collective-permute-start(f32[1,1024]{1,0:T(1,128)S(1)} %get-tuple-element.63), channel_id=1, source_target_pairs={{0,1},{1,2},{2,3},{3,4},{4,5},{5,6},{6,7},{7,8},{8,9},{9,10},{10,1... | collective-permute-start | bytes 12296 | tf_op jit(solution)/shard_map/ppermute | solution.py:304
  24.3 4.7 %collective-permute-start.3 = (f32[1,128]{1,0:T(1,128)S(1)}, f32[1,128]{1,0:T(1,128)S(1)}, u32[]{:S(2)}, u32[]{:S(2)}) collective-permute-start(f32[1,128]{1,0:T(1,128)S(1)} %get-tuple-element.71), channel_id=1, source_target_pairs={{0,4},{1,5},{2,6},{3,7},{4,0},{5,1},{6,2},{7,3},{8,12},{9,13},{10,... | collective-permute-start | bytes 1544 | tf_op jit(solution)/shard_map/ppermute | solution.py:411
  29.0 5.7 %collective-permute-start.4 = (f32[1,128]{1,0:T(1,128)S(1)}, f32[1,128]{1,0:T(1,128)S(1)}, u32[]{:S(2)}, u32[]{:S(2)}) collective-permute-start(f32[1,128]{1,0:T(1,128)S(1)} %add.15), channel_id=1, source_target_pairs={{0,12},{1,13},{2,14},{3,15},{4,8},{5,9},{6,10},{7,11},{8,4},{9,5},... | collective-permute-start | bytes 1544 | tf_op jit(solution)/shard_map/ppermute | solution.py:411
  34.7 3.5 %collective-permute-start.5 = (f32[1,128]{1,0:T(1,128)S(1)}, f32[1,128]{1,0:T(1,128)S(1)}, u32[]{:S(2)}, u32[]{:S(2)}) collective-permute-start(f32[1,128]{1,0:T(1,128)S(1)} %add.16), channel_id=1, source_target_pairs={{0,16},{1,17},{2,18},{3,19},{4,20},{5,21},{6,22},{7,23},{8,24},{9,... | collective-permute-start | bytes 1544 | tf_op jit(solution)/shard_map/ppermute | solution.py:411
  34.7 9.8 %collective-permute-start.10 = (bf16[2,256,256]{2,1,0:T(8,128)(2,1)S(1)}, bf16[2,256,256]{2,1,0:T(8,128)(2,1)S(1)}, u32[]{:S(2)}, u32[]{:S(2)}) collective-permute-start(bf16[2,256,256]{2,1,0:T(8,128)(2,1)S(1)} %get-tuple-element.101), channel_id=1, source_target_pairs={{0,2},{1,3},{2,4},{3,5},{4,6},{5,7},{6,8},{7,9},{8,10},{9,11},{10,... | collective-permute-start | bytes 786440 | tf_op jit(solution)/shard_map/ppermute | solution.py:304
  38.2 9.1 %collective-permute-start.9 = (bf16[2,256,256]{2,1,0:T(8,128)(2,1)S(1)}, bf16[2,256,256]{2,1,0:T(8,128)(2,1)S(1)}, u32[]{:S(2)}, u32[]{:S(2)}) collective-permute-start(bf16[2,256,256]{2,1,0:T(8,128)(2,1)S(1)} %get-tuple-element.100), channel_id=1, source_target_pairs={{0,1},{1,2},{2,3},{3,4},{4,5},{5,6},{6,7},{7,8},{8,9},{9,10},{10,1... | collective-permute-start | bytes 786440 | tf_op jit(solution)/shard_map/ppermute | solution.py:304
  38.2 4.8 %collective-permute-start.6 = (f32[1,128]{1,0:T(1,128)S(1)}, f32[1,128]{1,0:T(1,128)S(1)}, u32[]{:S(2)}, u32[]{:S(2)}) collective-permute-start(f32[1,128]{1,0:T(1,128)S(1)} %add.17), channel_id=1, source_target_pairs={{0,48},{1,49},{2,50},{3,51},{4,52},{5,53},{6,54},{7,55},{8,56},{9,... | collective-permute-start | bytes 1544 | tf_op jit(solution)/shard_map/ppermute | solution.py:411
  43.0 1.1 %collective-permute-start.7 = (f32[1,128]{1,0:T(1,128)S(1)}, f32[1,128]{1,0:T(1,128)S(1)}, u32[]{:S(2)}, u32[]{:S(2)}) collective-permute-start(f32[1,128]{1,0:T(1,128)S(1)} %add.18), channel_id=1, source_target_pairs={{0,1},{1,0},{2,3},{3,2},{4,5},{5,4},{6,7},{7,6},{8,9},{9,8},{10,11... | collective-permute-start | bytes 1544 | tf_op jit(solution)/shard_map/ppermute | solution.py:411
  44.1 4.3 %collective-permute-start.8 = (f32[1,128]{1,0:T(1,128)S(1)}, f32[1,128]{1,0:T(1,128)S(1)}, u32[]{:S(2)}, u32[]{:S(2)}) collective-permute-start(f32[1,128]{1,0:T(1,128)S(1)} %add.19.mine), channel_id=1, source_target_pairs={{0,2},{1,3},{2,0},{3,1},{4,6},{5,7},{6,4},{7,5},{8,10},{9,11},{10,... | collective-permute-start | bytes 1544 | tf_op jit(solution)/shard_map/ppermute | solution.py:432
